TPU v7x, 256 devices: a whole 4x4x8 slice. The times are simulated.
256 devices in a mesh: rows: 32 (over z_hi, y, core), cols: 8 (over x, z_lo).
Axes of the slice: x: 4, y: 4, z: 8 (z_hi: 4, z_lo: 2; z = z_hi * 2 + z_lo), core: 2. Of those that a mesh axis runs over, the one named last changes fastest.
Arguments:
- pair: bfloat16 [768, 768, 128], P('rows', 'cols'), may hold values from -6 to 6
- token_mask: int32 [768], P('cols'), may hold values from 0 to 1
- norm_gain: float32 [128], replicated, may hold values from 0.25 to 1.75
- norm_shift: float32 [128], replicated, may hold values from -3 to 3
- in_weight: bfloat16 [128, 512], replicated, may hold values from -1.5 to 1.5
- gate_bias: float32 [128], replicated, may hold values from -4 to 4
- bias_weight: bfloat16 [128, 4], replicated, may hold values from -16 to 16
- out_weight: bfloat16 [128, 128], replicated, may hold values from -1.5 to 1.5
- out_bias: float32 [128], replicated, may hold values from -1.8 to 1.8
Outputs:
- updated: bfloat16 [768, 768, 128], P('rows', 'cols')
All inputs are finite; a program needn't handle non-finite values.
Results may differ from a plain program's by a relative error of at most 0.006.
The roundings to bfloat16 on the way count: a program that leaves them out, or rounds other values in their place, can miss the bound.
Values may be sent and summed in bfloat16 or wider, within the bound.
A program may use at most 128 MiB of HBM per device.

v0:
```python
import jax
import jax.numpy as jnp
from jax import lax
from jax.sharding import PartitionSpec as P


def broadcast(x, axis, root):
    mine = lax.axis_index(axis) == root
    return lax.psum(jnp.where(mine, x, jnp.zeros_like(x)), axis)


def layer_norm(pair_block, norm_gain, norm_shift):
    as_float = pair_block.astype(jnp.float32)
    center = jnp.mean(as_float, axis=-1, keepdims=True)
    spread = jnp.mean(jnp.square(as_float - center), axis=-1, keepdims=True)
    return ((as_float - center) * lax.rsqrt(spread + 1e-05) * norm_gain + norm_shift).astype(
        jnp.bfloat16
    )


def shards(
    pair, token_mask, norm_gain, norm_shift, in_weight, gate_bias, bias_weight, out_weight, out_bias
):
    row_count, col_count, channels = pair.shape
    head_count = bias_weight.shape[1]
    inner_width = out_weight.shape[0]
    head_size = inner_width // head_count
    normed = layer_norm(pair, norm_gain, norm_shift)
    flat_normed = normed.reshape(row_count * col_count, channels)
    bias_tile = jnp.einsum(
        "jkc,ch->jhk", normed, bias_weight, preferred_element_type=jnp.float32
    ).astype(jnp.bfloat16)
    bias_rows_all = lax.all_gather(bias_tile, "cols", axis=2, tiled=True)
    groups = lax.axis_size("rows") // lax.axis_size("cols")
    first_root = lax.axis_index("cols") * groups
    pieces = []
    for offset in range(groups):
        pieces.append(broadcast(bias_rows_all, "rows", first_root + offset))
    own_bias = jnp.concatenate(pieces, axis=0)
    query_gate = jnp.concatenate(
        (in_weight[:, :inner_width], in_weight[:, 3 * inner_width :]), axis=1
    )
    projected = jnp.dot(flat_normed, query_gate, preferred_element_type=jnp.float32)
    queries = (projected[:, :inner_width] * head_size ** (-0.5)).astype(jnp.bfloat16)
    queries = queries.reshape(row_count, col_count, head_count, head_size)
    gates = jax.nn.sigmoid(projected[:, inner_width:] + gate_bias)
    key_value_weight = in_weight[:, inner_width : 3 * inner_width]
    mask_row = token_mask.reshape(1, col_count)
    start_state = (
        jnp.full((row_count, col_count, head_count), -jnp.inf, jnp.float32),
        jnp.zeros((row_count, col_count, head_count), jnp.float32),
        jnp.zeros((row_count, col_count, inner_width), jnp.float32),
    )
    key_values = jnp.dot(flat_normed, key_value_weight, preferred_element_type=jnp.float32).astype(
        jnp.bfloat16
    )
    key_values = key_values.reshape(row_count, col_count, 2 * inner_width)
    pair_keys = lax.all_gather(key_values, "cols", axis=1, tiled=True)
    mask_in = lax.all_gather(mask_row, "cols", axis=1, tiled=True)
    state_now = start_state
    begin_at = jnp.int32(0)
    span_len = pair_keys.shape[1]
    for low_edge in range(0, span_len, col_count):
        high_edge = min(low_edge + col_count, span_len)
        attend_pair_keys = pair_keys[:, low_edge:high_edge]
        attend_begin_at = begin_at + low_edge
        attend_running_max, attend_totals, attend_summed = state_now
        attend_span_len = attend_pair_keys.shape[1]
        key_part = attend_pair_keys[..., :inner_width].reshape(
            row_count, attend_span_len, head_count, head_size
        )
        value_part = attend_pair_keys[..., inner_width:].reshape(
            row_count, attend_span_len, head_count, head_size
        )
        scores = jnp.einsum(
            "rjhd,rkhd->rjhk", queries, key_part, preferred_element_type=jnp.float32
        )
        bias_part = lax.dynamic_slice_in_dim(own_bias, attend_begin_at, attend_span_len, 2).astype(
            jnp.float32
        )
        masking = 1000000000.0 * (mask_in[:, low_edge:high_edge][0].astype(jnp.float32) - 1.0)
        scores = scores + bias_part + masking
        new_max = jnp.maximum(attend_running_max, jnp.max(scores, axis=-1))
        shrink = jnp.exp(attend_running_max - new_max)
        weights = jnp.exp(scores - new_max[..., None])
        attend_totals = attend_totals * shrink + jnp.sum(weights, axis=-1)
        mixed_part = jnp.einsum(
            "rjhk,rkhd->rjhd",
            weights.astype(jnp.bfloat16),
            value_part,
            preferred_element_type=jnp.float32,
        )
        attend_summed = (
            attend_summed.reshape(row_count, col_count, head_count, head_size) * shrink[..., None]
            + mixed_part
        )
        state_now = (
            new_max,
            attend_totals,
            attend_summed.reshape(row_count, col_count, inner_width),
        )
    running_max, totals, summed = state_now
    attended = summed.reshape(row_count, col_count, head_count, head_size) / totals[..., None]
    gated = gates.reshape(row_count, col_count, head_count, head_size) * attended
    gated = gated.astype(jnp.bfloat16).reshape(row_count * col_count, inner_width)
    updated = jnp.dot(gated, out_weight, preferred_element_type=jnp.float32) + out_bias
    return updated.astype(jnp.bfloat16).reshape(row_count, col_count, channels)


def solution(mesh):
    placed = (P("rows", "cols", None), P("cols"), P(), P(), P(), P(), P(), P(), P())
    return jax.shard_map(
        shards, mesh=mesh, in_specs=placed, out_specs=P("rows", "cols", None), check_vma=False
    )
```

profile of v0, /device:TPU:2, one launch (start us, length us, event | category | flops | bytes accessed | tf_op | source)
XLA Modules:
  0.0 610.0 jit_solution(3657278403841043322)
XLA Ops:
  7.4 1.4 convert_reduce_fusion
  8.8 1.9 fusion.87
  10.7 1.8 fusion.90
  12.5 1.1 fusion.96
  13.8 30.4 %all_gather.10 = bf16[24,4,768]{0,1,2:T(4,128)(2,1)S(1)} all-gather(bf16[24,4,96]{0,1,2:T(4,128)(2,1)S(1)} %copy.144), channel_id=1, replica_groups=mesh['rows'=32,'cols'=8] {'cols'}, dimensions={2}, use_global_device_ids=true | all-gather | bytes 165888 | tf_op jit(solution)/shard_map/all_gather | solution.py:33
  44.7 0.8 broadcast_select_fusion
  45.6 1.5 convolution_convert_fusion
  48.2 1.2 reshape.410
  49.4 0.7 dynamic-slice
  51.0 10.0 %all-reduce = s32[768]{0:T(1024)S(1)} all-reduce(s32[768]{0:T(1024)S(1)} %dynamic-update-slice), channel_id=2, replica_groups=mesh['rows'=32,'cols'=8] {'cols'}, use_global_device_ids=true, to_apply=%add | all-reduce | flops 768 | bytes 6144
  61.0 1.4 copy.140
  62.4 2.4 reshape.407
  64.9 406.6 %all-reduce.4.cloned.1.call-done = (bf16[24,4,768]{2,0,1:T(8,128)(2,1)}, bf16[24,4,768]{2,0,1:T(8,128)(2,1)}, bf16[24,4,768]{2,0,1:T(8,128)(2,1)}, bf16[24,4,768]{2,0,1:T(8,128)(2,1)}) async-done(((bf16[24,4,768]{2,0,1:T(8,128)(2,1)}, bf16[24,4,768]{2,0,1:T(8,128)(2,1)}, bf16[24,4,768]{2,0,1:T(8,128)(2,1)}, bf16[24,4,768]{2,0,1:T(8,128)(2,1)}), (bf16[24,4,768]{2,0,1:T(8,128)(2,1)}, ...) | async-done | bytes 589840 | tf_op jit(solution)/shard_map/psum | solution.py:9
  471.5 0.9 constant_dynamic-update-slice_fusion.3
  472.4 0.9 constant_dynamic-update-slice_fusion.2
  473.3 0.9 constant_dynamic-update-slice_fusion.1
  474.3 0.9 constant_dynamic-update-slice_fusion
  475.2 1.0 slice_convert_fusion.6
  476.2 1.7 copy.169
  477.9 1.7 copy.164
  479.6 0.8 copy.159
  480.4 1.0 copy.149
  481.4 0.8 copy.154
  482.2 0.8 copy.174
  483.0 0.8 copy.179
  483.8 0.8 copy.184
  484.6 7.4 %fusion.145 = (bf16[24,96,128]{2,1,0:T(8,128)(2,1)}, bf16[24,96,128]{2,1,0:T(8,128)(2,1)}, bf16[24,96,128]{2,1,0:T(8,128)(2,1)S(1)}, bf16[24,96,128]{2,1,0:T(8,1...) fusion(bf16[24,768,256]{2,1,0:T(8,128)(2,1)} %all-gather.3.clon, ...), kind=kLoop, calls=%fused_computation.201 | loop fusion | bytes 18874368 | tf_op jit(solution)/shard_map/slice | solution.py:72
  492.0 2.2 copy.167
  494.2 2.3 copy.162
  496.5 2.2 copy.157
  498.7 2.2 copy.141
  500.9 2.2 copy.152
  503.2 2.2 copy.172
  505.4 2.2 copy.177
  507.6 1.2 copy.182
  508.8 1.4 copy.155
  510.3 4.6 fusion.29
  514.9 3.5 fusion.28
  518.4 3.4 fusion.27
  521.8 1.3 fusion.25
  523.2 1.3 fusion.26
  525.1 3.5 fusion.30
  528.6 3.5 fusion.31
  532.1 3.4 fusion.32
  535.4 0.7 fusion.144
  536.2 4.2 fusion.8
  540.4 2.2 fusion.45
  543.0 1.4 copy.165
  544.5 4.7 fusion.43
  549.2 6.5 %fusion.12 = (f32[24,96,4]{1,2,0:T(4,128)}, f32[24,96,4]{1,2,0:T(4,128)}) fusion(f32[24,4,96,96]{3,2,1,0:T(8,128)} %get-tuple-element.76, f32[24,96,4]{1,2,0:T(4,128)S(1)} %bitcast.267, f32[96]{0:T(128)S(1)} %get-tuple-element.63, f32[96,4,96]{0,2,1:T(8,128)S(1)} %copy-done.19, f32[24,96,4]{1,2,0:T(4,128)S(1)} %bitcast.263, f32[96]{0:T(128)S(1)} %get-tuple-element.62, ...), kind=kLoop, calls=%fused_computation.28 | loop fusion | flops 7059456 | bytes 7521024 | tf_op jit(solution)/shard_map/reduce_sum | solution.py:86
  555.7 2.3 fusion.41
  557.9 1.4 copy.170
  559.4 1.4 copy.175
  560.9 4.8 fusion.39
  565.7 6.7 %fusion.16 = (f32[24,96,4]{1,2,0:T(4,128)}, f32[24,96,4]{1,2,0:T(4,128)}) fusion(f32[24,4,96,96]{3,2,1,0:T(8,128)} %get-tuple-element.72, f32[24,96,4]{1,2,0:T(4,128)S(1)} %bitcast.261, f32[96]{0:T(128)S(1)} %get-tuple-element.61, f32[96,4,96]{0,2,1:T(8,128)S(1)} %copy-done.13, f32[24,96,4]{1,2,0:T(4,128)S(1)} %bitcast.257, f32[96]{0:T(128)S(1)} %get-tuple-element.60, ...), kind=kLoop, calls=%fused_computation.32 | loop fusion | flops 7059456 | bytes 7521024 | tf_op jit(solution)/shard_map/reduce_sum | solution.py:86
  572.4 2.3 fusion.37
  574.6 1.4 copy.180
  576.1 1.4 copy.185
  577.6 4.7 fusion.35
  582.2 6.3 %fusion.20 = (f32[24,96,4]{1,2,0:T(4,128)}, f32[24,96,4]{1,2,0:T(4,128)}) fusion(f32[24,4,96,96]{3,2,1,0:T(8,128)} %get-tuple-element.68, f32[24,96,4]{1,2,0:T(4,128)S(1)} %bitcast.255, f32[96]{0:T(128)S(1)} %get-tuple-element.59, f32[96,4,96]{0,2,1:T(8,128)S(1)} %copy-done.12, f32[24,96,4]{1,2,0:T(4,128)S(1)} %bitcast.251, f32[96]{0:T(128)S(1)} %get-tuple-element.58, ...), kind=kLoop, calls=%fused_computation.36 | loop fusion | flops 7059456 | bytes 7521024 | tf_op jit(solution)/shard_map/reduce_sum | solution.py:86
  588.6 2.2 fusion.33
  591.3 1.2 multiply_add_fusion
  592.5 7.6 %fusion.75 = bf16[24,96,4,32]{1,3,2,0:T(8,128)(2,1)S(1)} fusion(f32[24,4,32,96]{3,2,1,0:T(8,128)} %fusion.33, f32[24,4,32,96]{3,2,1,0:T(8,128)} %fusion.35, f32[24,4,32,96]{3,2,1,0:T(8,128)} %fusion.37, f32[24,4,32,96]{3,2,1,0:T(8,128)} %fusion.39, f32[24,4,32,96]{3,2,1,0:T(8,128)} %fusion.41, f32[24,4,32,96]{3,2,1,0:T(8,128)} %fusion.43, ...), kind=kOutput, calls=%fused_computation.86 | convolution fusion | flops 65470464 | bytes 14672256 | tf_op jit(solution)/shard_map/rjhk,rkhd->rjhd/dot_general | solution.py:87
  601.2 1.2 fusion.24
  (110 shorter events, 4.7 us)
Async XLA Ops:
  7.4 593.8 %copy-start = (bf16[128,128]{1,0:T(8,128)(2,1)S(1)}, bf16[128,128]{1,0:T(8,128)(2,1)}, u32[]{:S(2)}) copy-start(bf16[128,128]{1,0:T(8,128)(2,1)} %param.16) | copy-start | bytes 98308
  7.4 38.2 %copy-start.32 = (bf16[128,512]{1,0:T(8,128)(2,1)S(1)}, bf16[128,512]{1,0:T(8,128)(2,1)}, u32[]{:S(2)}) copy-start(bf16[128,512]{1,0:T(8,128)(2,1)} %param.13) | copy-start | bytes 393220
  7.4 464.1 %all-reduce.4.cloned.1.call-start = ((), (), s32[]{:S(2)}) async-start(), calls=%async_computation.1 | async-start | bytes 1179648 | tf_op jit(solution)/shard_map/psum | solution.py:9
  13.6 34.0 %copy-start.33 = (f32[128]{0:T(128)S(1)}, f32[128]{0:T(128)}, u32[]{:S(2)}) copy-start(f32[128]{0:T(128)} %param.14) | copy-start | bytes 1540
  45.5 439.0 %all-gather.3.cloned.1.call-start = ((), (), s32[]{:S(2)}) async-start(), calls=%async_computation | async-start | bytes 10616832 | tf_op jit(solution)/shard_map/all_gather | solution.py:58
  47.1 2.3 copy-start.36
  47.1 3.6 copy-start.35
  510.3 4.6 copy-start.8
  510.3 4.6 copy-start.16
  514.9 3.5 copy-start.7
  514.9 3.5 copy-start.18
  518.4 3.4 copy-start.6
  521.8 1.4 copy-start.5
  521.8 1.4 copy-start.20
  523.2 13.0 %copy-start.1 = (f32[24,4,96,96]{3,2,1,0:T(8,128)}, f32[24,4,96,96]{3,2,1,0:T(8,128)S(1)}, u32[]{:S(2)}) copy-start(f32[24,4,96,96]{3,2,1,0:T(8,128)S(1)} %get-tuple-element.78) | copy-start | bytes 10616836
  523.2 1.7 copy-start.4
  523.2 1.9 copy-start.14
  524.5 4.0 copy-start.3
  524.5 4.0 copy-start.11
  528.5 3.5 copy-start.2
  528.5 3.5 copy-start.9
  536.1 4.2 copy-start.31
  540.4 2.2 copy-start.22
  544.4 4.8 copy-start.17
  544.4 4.8 copy-start.19
  544.4 4.8 copy-start.27
  544.4 4.8 copy-start.29
  544.5 11.2 %slice-start.4 = ((s8[4718592]{0:T(1024)(128)(4,1)}), s8[4194304]{0:T(1024)(128)(4,1)S(1)}, s32[]{:S(2)}) async-start(s8[4718592]{0:T(1024)(128)(4,1)} %bitcast.229), calls=%async_computation.6 | async-start | bytes 8388608
  549.2 6.5 %slice-start.5 = ((s8[4718592]{0:T(1024)(128)(4,1)}), s8[524288]{0:T(1024)(128)(4,1)S(1)}, s32[]{:S(2)}) async-start(s8[4718592]{0:T(1024)(128)(4,1)} %bitcast.229), calls=%async_computation.7 | async-start | bytes 1048576
  560.8 4.8 copy-start.13
  560.9 4.8 copy-start.15
  560.9 4.8 copy-start.23
  560.9 4.8 copy-start.25
  560.9 11.5 %slice-start.2 = ((s8[4718592]{0:T(1024)(128)(4,1)}), s8[4194304]{0:T(1024)(128)(4,1)S(1)}, s32[]{:S(2)}) async-start(s8[4718592]{0:T(1024)(128)(4,1)} %bitcast.227), calls=%async_computation.4 | async-start | bytes 8388608
  565.7 6.7 %slice-start.3 = ((s8[4718592]{0:T(1024)(128)(4,1)}), s8[524288]{0:T(1024)(128)(4,1)S(1)}, s32[]{:S(2)}) async-start(s8[4718592]{0:T(1024)(128)(4,1)} %bitcast.227), calls=%async_computation.5 | async-start | bytes 1048576
  577.5 4.7 copy-start.10
  577.5 4.7 copy-start.12
  577.5 11.1 %slice-start = ((s8[4718592]{0:T(1024)(128)(4,1)}), s8[4194304]{0:T(1024)(128)(4,1)S(1)}, s32[]{:S(2)}) async-start(s8[4718592]{0:T(1024)(128)(4,1)} %bitcast.225), calls=%async_computation.2 | async-start | bytes 8388608
  582.2 6.4 %slice-start.1 = ((s8[4718592]{0:T(1024)(128)(4,1)}), s8[524288]{0:T(1024)(128)(4,1)S(1)}, s32[]{:S(2)}) async-start(s8[4718592]{0:T(1024)(128)(4,1)} %bitcast.225), calls=%async_computation.3 | async-start | bytes 1048576
  588.6 2.3 copy-start.21
  588.6 2.7 copy-start.24
  588.6 2.7 copy-start.26
  588.6 2.7 copy-start.28
  588.6 2.7 copy-start.30
  592.5 8.7 %copy-start.34 = (f32[128]{0:T(128)S(1)}, f32[128]{0:T(128)}, u32[]{:S(2)}) copy-start(f32[128]{0:T(128)} %param.17) | copy-start | bytes 1540
Sparse Core Ops, SparseCore 0:
  45.7 425.7 all-reduce.3
Sparse Core Ops, SparseCore 1:
  47.8 195.4 all-gather.2
where the time goes:
time: 617 us; the launch traced here: 610 us
  waiting for transfers between devices  407 us (66%)
  matrix products  59.2 us (10%)
  local copies, waits for them, and re-layouts  54.4 us (9%)
  blocking collectives  40.4 us (7%)
  other arithmetic  32.8 us (5%)
  between operations  16.5 us (3%)
    psum x1, waiting for transfers between devices, broadcast(): return lax.psum(jnp.where(mine, x, jnp.zeros_like(x)), axis)  407 us
    dot_general x8, matrix products, shards(): jnp.einsum('rjhk,rkhd->rjhd', weights.astype(jnp.bfloat16), value_part, p...  30.7 us
    all_gather x1, blocking collectives, shards(): bias_rows_all = lax.all_gather(bias_tile, 'cols', axis=2, tiled=True)  30.4 us
    dot_general x8, matrix products, shards(): jnp.einsum('rjhd,rkhd->rjhk', queries, key_part, preferred_element_type=j...  24.3 us
    reduce_sum x4, other arithmetic, shards(): attend_totals = attend_totals * shrink + jnp.sum(weights, axis=-1)  23.7 us
    slice x8, local copies, waits for them, and re-layouts, shards(): attend_pair_keys[..., :inner_width]  16.8 us
    slice x9, local copies, waits for them, and re-layouts, shards(): attend_pair_keys[..., inner_width:]  16.8 us
  transfers between devices with their start and end apart: 2, of which 1 were waited for; matrix products, arithmetic and copies ran while one was open for 4% of the time, Pallas kernels for 0%

commit v1 on v0

v1 whole, which is shorter than its diff:
```python
import functools

import jax
import jax.numpy as jnp
from jax import lax
from jax.experimental import pallas as pl
from jax.experimental.pallas import tpu as pltpu
from jax.sharding import PartitionSpec as P


def layer_norm(pair_block, norm_gain, norm_shift):
    as_float = pair_block.astype(jnp.float32)
    center = jnp.mean(as_float, axis=-1, keepdims=True)
    spread = jnp.mean(jnp.square(as_float - center), axis=-1, keepdims=True)
    return ((as_float - center) * lax.rsqrt(spread + 1e-05) * norm_gain + norm_shift).astype(
        jnp.bfloat16
    )


def attend_kernel(
    head_count,
    head_size,
    own_ref,
    all_ref,
    bias_ref,
    mask_ref,
    wqg_ref,
    wkv_ref,
    gb_ref,
    ow_ref,
    ob_ref,
    out_ref,
):
    inner = head_count * head_size
    own = own_ref[0]
    qg = jnp.dot(own, wqg_ref[...], preferred_element_type=jnp.float32)
    queries = (qg[:, :inner] * head_size ** (-0.5)).astype(jnp.bfloat16)
    gates = jax.nn.sigmoid(qg[:, inner:] + gb_ref[...])
    row = all_ref[0]
    kv = jnp.dot(row, wkv_ref[...], preferred_element_type=jnp.float32)
    keys = kv[:, :inner].astype(jnp.bfloat16)
    values = kv[:, inner:].astype(jnp.bfloat16)
    lane_head = lax.broadcasted_iota(jnp.int32, (1, inner), 1) // head_size
    masking = mask_ref[...]
    attended = jnp.zeros((own.shape[0], inner), jnp.float32)
    for h in range(head_count):
        in_head = lane_head == h
        q_h = jnp.where(in_head, queries, jnp.zeros_like(queries))
        scores = lax.dot_general(
            q_h, keys, (((1,), (1,)), ((), ())), preferred_element_type=jnp.float32
        )
        scores = scores + bias_ref[h].astype(jnp.float32)
        scores = scores + masking
        top = jnp.max(scores, axis=-1, keepdims=True)
        expo = jnp.exp(scores - top)
        totals = jnp.sum(expo, axis=-1, keepdims=True)
        mixed = jnp.dot(expo.astype(jnp.bfloat16), values, preferred_element_type=jnp.float32)
        attended = jnp.where(in_head, mixed / totals, attended)
    gated = (gates * attended).astype(jnp.bfloat16)
    updated = jnp.dot(gated, ow_ref[...], preferred_element_type=jnp.float32) + ob_ref[...]
    out_ref[0] = updated.astype(out_ref.dtype)


def attend(normed, normed_all, bias, masking, wqg, wkv, gate_bias, out_weight, out_bias):
    row_count, col_count, channels = normed.shape
    span = normed_all.shape[1]
    head_count = bias.shape[0]
    inner = out_weight.shape[0]
    head_size = inner // head_count
    const2 = lambda i: (0, 0)
    return pl.pallas_call(
        functools.partial(attend_kernel, head_count, head_size),
        out_shape=jax.ShapeDtypeStruct((row_count, col_count, channels), jnp.bfloat16),
        grid=(row_count,),
        in_specs=[
            pl.BlockSpec((1, col_count, channels), lambda i: (i, 0, 0)),
            pl.BlockSpec((1, span, channels), lambda i: (i, 0, 0)),
            pl.BlockSpec((head_count, col_count, span), lambda i: (0, 0, 0)),
            pl.BlockSpec((1, span), const2),
            pl.BlockSpec(wqg.shape, const2),
            pl.BlockSpec(wkv.shape, const2),
            pl.BlockSpec((1, inner), const2),
            pl.BlockSpec(out_weight.shape, const2),
            pl.BlockSpec((1, channels), const2),
        ],
        out_specs=pl.BlockSpec((1, col_count, channels), lambda i: (i, 0, 0)),
    )(
        normed,
        normed_all,
        bias,
        masking,
        wqg,
        wkv,
        gate_bias.reshape(1, inner),
        out_weight,
        out_bias.reshape(1, channels),
    )


def shards(
    pair, token_mask, norm_gain, norm_shift, in_weight, gate_bias, bias_weight, out_weight, out_bias
):
    inner = out_weight.shape[0]
    normed = layer_norm(pair, norm_gain, norm_shift)
    bias_tile = jnp.einsum(
        "jkc,ch->hjk", normed, bias_weight, preferred_element_type=jnp.float32
    ).astype(jnp.bfloat16)
    bias_cols = lax.all_gather(bias_tile, "rows", axis=1, tiled=True)
    bias = lax.all_to_all(bias_cols, "cols", 1, 2, tiled=True)
    normed_all = lax.all_gather(normed, "cols", axis=1, tiled=True)
    mask_all = lax.all_gather(token_mask, "cols", axis=0, tiled=True)
    masking = (1000000000.0 * (mask_all.astype(jnp.float32) - 1.0)).reshape(1, -1)
    wqg = jnp.concatenate((in_weight[:, :inner], in_weight[:, 3 * inner :]), axis=1)
    wkv = in_weight[:, inner : 3 * inner]
    return attend(normed, normed_all, bias, masking, wqg, wkv, gate_bias, out_weight, out_bias)


def solution(mesh):
    placed = (P("rows", "cols", None), P("cols"), P(), P(), P(), P(), P(), P(), P())
    return jax.shard_map(
        shards, mesh=mesh, in_specs=placed, out_specs=P("rows", "cols", None), check_vma=False
    )
```

time: 617 us -> 186 us (0.30)
  the two profiles are of different devices: /device:TPU:2 before, /device:TPU:64 now
where the time goes in v1:
time: 186 us; the launch traced here: 184 us
  blocking collectives  71.9 us (39%)
  Pallas kernels  46.6 us (25%)
  waiting for transfers between devices  36 us (19%)
  between operations  14.2 us (8%)
  other arithmetic  5.45 us (3%)
  starting transfers between devices  4.34 us (2%)
  local copies, waits for them, and re-layouts  4.07 us (2%)
    pallas_call x1, Pallas kernels, attend(): pl.pallas_call(functools.partial(attend_kernel, head_count, head_size), o...  46.6 us
    all_gather x1, blocking collectives, shards(): bias_cols = lax.all_gather(bias_tile, 'rows', axis=1, tiled=True)  45.9 us
    all_gather x1, waiting for transfers between devices, shards(): normed_all = lax.all_gather(normed, 'cols', axis=1, tiled=True)  36 us
    unnamed x1, blocking collectives  26.1 us
    all_to_all x1, starting transfers between devices, shards(): bias = lax.all_to_all(bias_cols, 'cols', 1, 2, tiled=True)  4.31 us
  transfers between devices with their start and end apart: 2, of which 1 were waited for; matrix products, arithmetic and copies ran while one was open for 3% of the time, Pallas kernels for 0%

profile of v1, /device:TPU:64, one launch (start us, length us, event | category | flops | bytes accessed | tf_op | source)
XLA Modules:
  0.0 184.1 jit_solution(2886626742889234043)
XLA Ops:
  6.5 0.0 copy-start
  6.5 0.0 copy-start.1
  6.5 0.0 copy-start.4
  6.5 0.0 copy-start.3
  6.5 0.0 all-gather.2.cloned.1.call-start
  6.6 1.4 convert_reduce_fusion
  8.0 1.9 %fusion.2 = f32[24,96]{1,0:T(8,128)S(1)} fusion(bf16[24,96,128]{2,1,0:T(8,128)(2,1)} %param.9, f32[24,96]{1,0:T(8,128)S(1)} %broadcast_multiply_fusion), kind=kLoop, calls=%fused_computation.4 | loop fusion | flops 1177344 | bytes 608256 | tf_op jit(solution)/shard_map/reduce_sum | solution.py:14
  9.9 0.0 copy-done.1
  9.9 0.0 copy-done.4
  9.9 0.0 copy-done.3
  9.9 1.5 fusion.5.own_ref
  11.4 0.0 all-gather.2.cloned.1.call-update
  11.5 0.0 copy-done
  11.5 1.5 fusion.6
  13.0 0.0 copy-start.2
  13.0 0.0 copy-start.6
  13.0 0.0 copy-start.5
  13.0 45.9 %all_gather.10 = bf16[4,768,96]{2,0,1:T(4,128)(2,1)} all-gather(bf16[4,24,96]{2,0,1:T(4,128)(2,1)S(1)} %fusion.6), channel_id=1, replica_groups=mesh['rows'=32,'cols'=8] {'rows'}, dimensions={1}, use_global_device_ids=true | all-gather | bytes 608256 | tf_op jit(solution)/shard_map/all_gather | solution.py:108
  58.9 4.3 %all-to-all-start = ((bf16[4,768,96]{2,0,1:T(4,128)(2,1)}), bf16[4,768,96]{2,0,1:T(4,128)(2,1)S(1)}, u32[]{:S(2)}, u32[]{:S(2)}) async-start(bf16[4,768,96]{2,0,1:T(4,128)(2,1)} %all_gather.10), calls=%async_computation | async-start | bytes 1572864 | tf_op jit(solution)/shard_map/all_to_all | solution.py:109
  63.2 0.0 copy-done.2
  63.2 0.6 slice.11.wkv_ref
  63.8 0.0 copy-done.6
  63.8 0.6 dynamic-slice
  65.1 0.0 copy-done.5
  65.1 0.2 dynamic-update-slice
  65.3 26.1 %all-reduce = s32[768]{0:T(1024)S(1)} all-reduce(s32[768]{0:T(1024)S(1)} %dynamic-update-slice), channel_id=1, replica_groups=mesh['rows'=32,'cols'=8] {'cols'}, use_global_device_ids=true, to_apply=%add | all-reduce | flops 768 | bytes 6144
  91.4 0.6 reshape.23.mask_ref
  92.0 0.6 pad_maximum_fusion.wqg_ref
  92.7 0.0 all-to-all-done
  92.7 0.5 copy.13
  93.2 1.5 all_to_all.16.bias_ref
  94.6 36.0 %all-gather.2.cloned.1.call-done.all_ref = bf16[24,768,128]{2,1,0:T(8,128)(2,1)} async-done(((bf16[24,96,128]{2,1,0:T(8,128)(2,1)}), bf16[24,768,128]{2,1,0:T(8,128)(2,1)}) %all-gather.2.cloned.1.call-update) | async-done | bytes 4718608 | tf_op jit(solution)/shard_map/all_gather | solution.py:110
  130.6 46.6 %shard_map.91 = bf16[24,96,128]{2,1,0:T(8,128)(2,1)} custom-call(bf16[24,96,128]{2,1,0:T(8,128)(2,1)} %fusion.5.own_ref, bf16[24,768,128]{2,1,0:T(8,128)(2,1)} %all-gather.2.cloned.1.call-done.all_ref, bf16[4,96,768]{2,1,0:T(8,128)(2,1)} %all_to_all.16.bias_ref, f32[1,768]{1,0:T(1,128)} %reshape.23.mask_ref, bf16[128,256]{1,0:T(8,128)(2,1)} %pad_maximum_fusion.wqg_ref, ...), custom_call_target="tpu_custom_call" | custom-call | tf_op jit(solution)/shard_map/pallas_call | solution.py:71
  (5 shorter events, 0.0 us)
Async XLA Ops:
  6.5 4.9 %copy-start = (bf16[128,4]{0,1:T(4,128)(2,1)S(1)}, bf16[128,4]{0,1:T(4,128)(2,1)}, u32[]{:S(2)}) copy-start(bf16[128,4]{0,1:T(4,128)(2,1)} %param.15) | copy-start | bytes 3076
  6.5 3.4 %copy-start.1 = (bf16[24,96,128]{2,1,0:T(8,128)(2,1)S(1)}, bf16[24,96,128]{2,1,0:T(8,128)(2,1)}, u32[]{:S(2)}) copy-start(bf16[24,96,128]{2,1,0:T(8,128)(2,1)} %param.9) | copy-start | bytes 1769476
  6.5 3.4 %copy-start.4 = (f32[128]{0:T(128)S(1)}, f32[128]{0:T(128)}, u32[]{:S(2)}) copy-start(f32[128]{0:T(128)} %param.11) | copy-start | bytes 1540
  6.5 3.4 %copy-start.3 = (f32[128]{0:T(128)S(1)}, f32[128]{0:T(128)}, u32[]{:S(2)}) copy-start(f32[128]{0:T(128)} %param.12) | copy-start | bytes 1540
  6.5 124.1 %all-gather.2.cloned.1.call-start = ((), (), s32[]{:S(2)}) async-start(), calls=%async_computation.1 | async-start | bytes 5308416 | tf_op jit(solution)/shard_map/all_gather | solution.py:110
  13.0 50.2 %copy-start.2 = (bf16[128,512]{1,0:T(8,128)(2,1)S(1)}, bf16[128,512]{1,0:T(8,128)(2,1)}, u32[]{:S(2)}) copy-start(bf16[128,512]{1,0:T(8,128)(2,1)} %param.13) | copy-start | bytes 393220
  13.0 50.8 %copy-start.6 = (u32[256]{0:T(256)S(1)}, u32[256]{0:T(256)}, u32[]{:S(2)}) copy-start(u32[256]{0:T(256)} %constant.16) | copy-start | bytes 3076
  13.0 52.1 %copy-start.5 = (s32[96]{0:T(128)S(1)}, s32[96]{0:T(128)}, u32[]{:S(2)}) copy-start(s32[96]{0:T(128)} %param.10) | copy-start | bytes 1156
  58.9 33.8 %all-to-all-start = ((bf16[4,768,96]{2,0,1:T(4,128)(2,1)}), bf16[4,768,96]{2,0,1:T(4,128)(2,1)S(1)}, u32[]{:S(2)}, u32[]{:S(2)}) async-start(bf16[4,768,96]{2,0,1:T(4,128)(2,1)} %all_gather.10), calls=%async_computation | async-start | bytes 1572864 | tf_op jit(solution)/shard_map/all_to_all | solution.py:109
Sparse Core Ops, SparseCore 0:
  11.6 118.9 all-gather.1

commit v2 on v1

--- a/solution.py
+++ b/solution.py
@@ -6,6 +6,9 @@
 from jax.experimental import pallas as pl
 from jax.experimental.pallas import tpu as pltpu
 from jax.sharding import PartitionSpec as P
+
+
+CHUNKS = 4
 
 
 def layer_norm(pair_block, norm_gain, norm_shift):
@@ -23,7 +26,6 @@
     own_ref,
     all_ref,
     bias_ref,
-    mask_ref,
     wqg_ref,
     wkv_ref,
     gb_ref,
@@ -41,7 +43,7 @@
     keys = kv[:, :inner].astype(jnp.bfloat16)
     values = kv[:, inner:].astype(jnp.bfloat16)
     lane_head = lax.broadcasted_iota(jnp.int32, (1, inner), 1) // head_size
-    masking = mask_ref[...]
+    masking = 1000000000.0 * (bias_ref[head_count, 0:1, :].astype(jnp.float32) - 1.0)
     attended = jnp.zeros((own.shape[0], inner), jnp.float32)
     for h in range(head_count):
         in_head = lane_head == h
@@ -61,10 +63,10 @@
     out_ref[0] = updated.astype(out_ref.dtype)
 
 
-def attend(normed, normed_all, bias, masking, wqg, wkv, gate_bias, out_weight, out_bias):
+def attend(normed, normed_all, bias, wqg, wkv, gate_bias, out_weight, out_bias):
     row_count, col_count, channels = normed.shape
     span = normed_all.shape[1]
-    head_count = bias.shape[0]
+    head_count = bias.shape[0] - 1
     inner = out_weight.shape[0]
     head_size = inner // head_count
     const2 = lambda i: (0, 0)
@@ -75,8 +77,7 @@
         in_specs=[
             pl.BlockSpec((1, col_count, channels), lambda i: (i, 0, 0)),
             pl.BlockSpec((1, span, channels), lambda i: (i, 0, 0)),
-            pl.BlockSpec((head_count, col_count, span), lambda i: (0, 0, 0)),
-            pl.BlockSpec((1, span), const2),
+            pl.BlockSpec((head_count + 1, col_count, span), lambda i: (0, 0, 0)),
             pl.BlockSpec(wqg.shape, const2),
             pl.BlockSpec(wkv.shape, const2),
             pl.BlockSpec((1, inner), const2),
@@ -88,7 +89,6 @@
         normed,
         normed_all,
         bias,
-        masking,
         wqg,
         wkv,
         gate_bias.reshape(1, inner),
@@ -105,14 +105,24 @@
     bias_tile = jnp.einsum(
         "jkc,ch->hjk", normed, bias_weight, preferred_element_type=jnp.float32
     ).astype(jnp.bfloat16)
-    bias_cols = lax.all_gather(bias_tile, "rows", axis=1, tiled=True)
+    mask_tile = jnp.broadcast_to(
+        token_mask.astype(jnp.bfloat16)[None, None, :], (1,) + bias_tile.shape[1:]
+    )
+    payload = jnp.concatenate((bias_tile, mask_tile), axis=0)
+    bias_cols = lax.all_gather(payload, "rows", axis=1, tiled=True)
     bias = lax.all_to_all(bias_cols, "cols", 1, 2, tiled=True)
-    normed_all = lax.all_gather(normed, "cols", axis=1, tiled=True)
-    mask_all = lax.all_gather(token_mask, "cols", axis=0, tiled=True)
-    masking = (1000000000.0 * (mask_all.astype(jnp.float32) - 1.0)).reshape(1, -1)
     wqg = jnp.concatenate((in_weight[:, :inner], in_weight[:, 3 * inner :]), axis=1)
     wkv = in_weight[:, inner : 3 * inner]
-    return attend(normed, normed_all, bias, masking, wqg, wkv, gate_bias, out_weight, out_bias)
+    row_count = normed.shape[0]
+    chunk = row_count // CHUNKS
+    outs = []
+    for q in range(CHUNKS):
+        part = normed[q * chunk : (q + 1) * chunk]
+        part_all = lax.all_gather(part, "cols", axis=1, tiled=True)
+        outs.append(
+            attend(part, part_all, bias, wqg, wkv, gate_bias, out_weight, out_bias)
+        )
+    return jnp.concatenate(outs, axis=0)
 
 
 def solution(mesh):

time: 186 us -> 216 us (1.16)
  waiting for transfers between devices: 36 us -> 85 us
  blocking collectives: 71.9 us -> 43.8 us
  Pallas kernels: 46.6 us -> 52.2 us
  local copies, waits for them, and re-layouts: 4.07 us -> 8.8 us
    all_gather x1 -> x4, waiting for transfers between devices: 36 us -> 66.6 us  [shards(): part_all = lax.all_gather(part, 'cols', axis=1, tiled=True)]
    unnamed x1 -> x0, blocking collectives: 26.1 us -> none
    all_to_all x1, waiting for transfers between devices: 0.01 us -> 16.5 us  [shards(): bias = lax.all_to_all(bias_cols, 'cols', 1, 2, tiled=True)]
    pallas_call x1 -> x4, Pallas kernels: 46.6 us -> 52.2 us  [attend(): pl.pallas_call(functools.partial(attend_kernel, head_count, head_size), o...]
    unnamed x17 -> x20, local copies, waits for them, and re-layouts: 0.86 us -> 4.18 us
  transfers between devices with their start and end apart: 2 -> 5, of which waited for: 1 -> 4; matrix products, arithmetic and copies ran while one was open for 3% -> 3% of each run, Pallas kernels for 0% -> 18%
where the time goes in v2:
time: 216 us; the launch traced here: 215 us
  waiting for transfers between devices  85 us (39%)
  Pallas kernels  52.2 us (24%)
  blocking collectives  43.8 us (20%)
  between operations  13.3 us (6%)
  local copies, waits for them, and re-layouts  8.8 us (4%)
  other arithmetic  6.6 us (3%)
  starting transfers between devices  5.25 us (2%)
    all_gather x4, waiting for transfers between devices, shards(): part_all = lax.all_gather(part, 'cols', axis=1, tiled=True)  66.6 us
    pallas_call x4, Pallas kernels, attend(): pl.pallas_call(functools.partial(attend_kernel, head_count, head_size), o...  52.2 us
    all_gather x1, blocking collectives, shards(): bias_cols = lax.all_gather(payload, 'rows', axis=1, tiled=True)  43.8 us
    all_to_all x1, waiting for transfers between devices, shards(): bias = lax.all_to_all(bias_cols, 'cols', 1, 2, tiled=True)  16.5 us
    all_to_all x1, starting transfers between devices, shards(): bias = lax.all_to_all(bias_cols, 'cols', 1, 2, tiled=True)  5.1 us
  transfers between devices with their start and end apart: 5, of which 4 were waited for; matrix products, arithmetic and copies ran while one was open for 3% of the time, Pallas kernels for 18%

profile of v2, /device:TPU:64, one launch (start us, length us, event | category | flops | bytes accessed | tf_op | source)
XLA Modules:
  0.0 215.4 jit_solution(6864826956371551414)
XLA Ops:
  6.5 0.0 copy-start
  6.5 0.0 copy-start.1
  6.5 0.0 copy-start.7
  6.5 0.0 copy-start.6
  6.5 0.0 all-gather.5.cloned.1.call-start
  6.6 1.4 convert_reduce_fusion
  8.0 1.9 fusion.2
  9.9 0.0 copy-done.1
  9.9 0.0 copy-done.7
  9.9 0.0 copy-done.6
  9.9 0.8 fusion.5
  10.8 0.0 copy-start.8
  10.8 0.8 fusion.8
  11.6 0.0 all-gather.5.cloned.1.call-update
  11.6 0.0 all-gather.7.cloned.1.call-start
  11.7 0.7 all-gather.7.cloned.1.call-update
  12.4 0.0 all-gather.9.cloned.1.call-start
  12.4 0.7 all-gather.9.cloned.1.call-update
  13.1 0.0 all-gather.11.cloned.1.call-start
  13.2 0.5 all-gather.11.cloned.1.call-update
  13.7 0.0 copy-done.8
  13.7 0.0 copy-done
  13.7 0.5 fusion.6
  14.3 43.8 %all_gather.16 = bf16[5,768,96]{2,1,0:T(8,128)(2,1)S(1)} all-gather(bf16[5,24,96]{2,1,0:T(8,128)(2,1)S(1)} %copy.13), channel_id=1, replica_groups=mesh['rows'=32,'cols'=8] {'rows'}, dimensions={1}, use_global_device_ids=true | all-gather | bytes 760320 | tf_op jit(solution)/shard_map/all_gather | solution.py:112
  58.0 0.7 copy.19
  58.8 2.5 %reshape.32 = bf16[8,2,23040]{2,1,0:T(2,128)(2,1)} reshape(bf16[768,5,96]{2,1,0:T(8,128)(2,1)S(1)} %bitcast.18) | data formatting | bytes 1474560
  61.2 0.0 copy-start.5
  61.2 5.1 %all-to-all-start = ((bf16[8,2,23040]{2,1,0:T(2,128)(2,1)}), bf16[8,2,23040]{2,1,0:T(2,128)(2,1)S(1)}, u32[]{:S(2)}, u32[]{:S(2)}) async-start(bf16[8,2,23040]{2,1,0:T(2,128)(2,1)} %reshape.32), calls=%async_computation | async-start | bytes 1474560 | tf_op jit(solution)/shard_map/all_to_all | solution.py:113
  66.3 0.0 copy-done.5
  66.3 0.6 slice.24.wkv_ref
  67.0 0.6 pad_maximum_fusion.1.wqg_ref
  67.6 16.5 %all-to-all-done = bf16[8,2,23040]{2,1,0:T(2,128)(2,1)S(1)} async-done(((bf16[8,2,23040]{2,1,0:T(2,128)(2,1)}), bf16[8,2,23040]{2,1,0:T(2,128)(2,1)S(1)}, u32[]{:S(2)}, u32[]{:S(2)}) %all-to-all-start) | async-done | bytes 737312 | tf_op jit(solution)/shard_map/all_to_all | solution.py:113
  84.1 1.7 reshape.33
  85.8 0.7 copy.18
  86.5 1.7 all_to_all.16.bias_ref
  88.2 0.0 all-gather.5.cloned.1.call-done.all_ref
  88.2 13.1 %shard_map.91 = bf16[6,96,128]{2,1,0:T(8,128)(2,1)} custom-call(bf16[6,96,128]{2,1,0:T(8,128)(2,1)} %get-tuple-element.5.own_ref, bf16[6,768,128]{2,1,0:T(8,128)(2,1)} %all-gather.5.cloned.1.call-done.all_ref, bf16[5,96,768]{2,1,0:T(8,128)(2,1)} %all_to_all.16.bias_ref, bf16[128,256]{1,0:T(8,128)(2,1)} %pad_maximum_fusion.1.wqg_ref, ...), custom_call_target="tpu_custom_call" | custom-call | tf_op jit(solution)/shard_map/pallas_call | solution.py:73
  101.3 4.1 %all-gather.7.cloned.1.call-done.all_ref = bf16[6,768,128]{2,1,0:T(8,128)(2,1)} async-done(((bf16[6,96,128]{2,1,0:T(8,128)(2,1)}), bf16[6,768,128]{2,1,0:T(8,128)(2,1)}) %all-gather.7.cloned.1.call-update) | async-done | bytes 1179664 | tf_op jit(solution)/shard_map/all_gather | solution.py:121
  105.4 13.1 %shard_map.92 = bf16[6,96,128]{2,1,0:T(8,128)(2,1)} custom-call(bf16[6,96,128]{2,1,0:T(8,128)(2,1)} %get-tuple-element.8.own_ref, bf16[6,768,128]{2,1,0:T(8,128)(2,1)} %all-gather.7.cloned.1.call-done.all_ref, bf16[5,96,768]{2,1,0:T(8,128)(2,1)} %all_to_all.16.bias_ref, bf16[128,256]{1,0:T(8,128)(2,1)} %pad_maximum_fusion.1.wqg_ref, ...), custom_call_target="tpu_custom_call" | custom-call | tf_op jit(solution)/shard_map/pallas_call | solution.py:73
  118.4 32.0 %all-gather.9.cloned.1.call-done.all_ref = bf16[6,768,128]{2,1,0:T(8,128)(2,1)} async-done(((bf16[6,96,128]{2,1,0:T(8,128)(2,1)}), bf16[6,768,128]{2,1,0:T(8,128)(2,1)}) %all-gather.9.cloned.1.call-update) | async-done | bytes 1179664 | tf_op jit(solution)/shard_map/all_gather | solution.py:121
  150.4 13.1 %shard_map.93 = bf16[6,96,128]{2,1,0:T(8,128)(2,1)} custom-call(bf16[6,96,128]{2,1,0:T(8,128)(2,1)} %get-tuple-element.7.own_ref, bf16[6,768,128]{2,1,0:T(8,128)(2,1)} %all-gather.9.cloned.1.call-done.all_ref, bf16[5,96,768]{2,1,0:T(8,128)(2,1)} %all_to_all.16.bias_ref, bf16[128,256]{1,0:T(8,128)(2,1)} %pad_maximum_fusion.1.wqg_ref, ...), custom_call_target="tpu_custom_call" | custom-call | tf_op jit(solution)/shard_map/pallas_call | solution.py:73
  163.5 0.0 copy-start.2
  163.5 0.0 copy-start.3
  163.5 0.0 copy-start.4
  163.5 30.5 %all-gather.11.cloned.1.call-done.all_ref = bf16[6,768,128]{2,1,0:T(8,128)(2,1)} async-done(((bf16[6,96,128]{2,1,0:T(8,128)(2,1)}), bf16[6,768,128]{2,1,0:T(8,128)(2,1)}) %all-gather.11.cloned.1.call-update) | async-done | bytes 1179664 | tf_op jit(solution)/shard_map/all_gather | solution.py:121
  193.9 13.1 %shard_map.94 = bf16[6,96,128]{2,1,0:T(8,128)(2,1)} custom-call(bf16[6,96,128]{2,1,0:T(8,128)(2,1)} %get-tuple-element.6.own_ref, bf16[6,768,128]{2,1,0:T(8,128)(2,1)} %all-gather.11.cloned.1.call-done.all_ref, bf16[5,96,768]{2,1,0:T(8,128)(2,1)} %all_to_all.16.bias_ref, bf16[128,256]{1,0:T(8,128)(2,1)} %pad_maximum_fusion.1.wqg_ref, ...), custom_call_target="tpu_custom_call" | custom-call | tf_op jit(solution)/shard_map/pallas_call | solution.py:73
  207.0 0.0 copy-done.2
  207.0 0.0 copy-done.3
  207.0 0.0 copy-done.4
  207.0 1.8 pad_maximum_fusion
  (7 shorter events, 0.1 us)
Async XLA Ops:
  6.5 7.2 %copy-start = (bf16[128,4]{0,1:T(4,128)(2,1)S(1)}, bf16[128,4]{0,1:T(4,128)(2,1)}, u32[]{:S(2)}) copy-start(bf16[128,4]{0,1:T(4,128)(2,1)} %param.15) | copy-start | bytes 3076
  6.5 3.4 %copy-start.1 = (bf16[24,96,128]{2,1,0:T(8,128)(2,1)S(1)}, bf16[24,96,128]{2,1,0:T(8,128)(2,1)}, u32[]{:S(2)}) copy-start(bf16[24,96,128]{2,1,0:T(8,128)(2,1)} %param.9) | copy-start | bytes 1769476
  6.5 3.4 %copy-start.7 = (f32[128]{0:T(128)S(1)}, f32[128]{0:T(128)}, u32[]{:S(2)}) copy-start(f32[128]{0:T(128)} %param.11) | copy-start | bytes 1540
  6.5 3.4 %copy-start.6 = (f32[128]{0:T(128)S(1)}, f32[128]{0:T(128)}, u32[]{:S(2)}) copy-start(f32[128]{0:T(128)} %param.12) | copy-start | bytes 1540
  6.5 81.6 %all-gather.5.cloned.1.call-start = ((), (), s32[]{:S(2)}) async-start(), calls=%async_computation.1 | async-start | bytes 1327104 | tf_op jit(solution)/shard_map/all_gather | solution.py:121
  10.8 2.9 %copy-start.8 = (s32[96]{0:T(128)S(1)}, s32[96]{0:T(128)}, u32[]{:S(2)}) copy-start(s32[96]{0:T(128)} %param.10) | copy-start | bytes 1156
  11.6 93.8 %all-gather.7.cloned.1.call-start = ((), (), s32[]{:S(2)}) async-start(), calls=%async_computation.2 | async-start | bytes 1327104 | tf_op jit(solution)/shard_map/all_gather | solution.py:121
  12.4 138.0 %all-gather.9.cloned.1.call-start = ((), (), s32[]{:S(2)}) async-start(), calls=%async_computation.3 | async-start | bytes 1327104 | tf_op jit(solution)/shard_map/all_gather | solution.py:121
  13.1 180.8 %all-gather.11.cloned.1.call-start = ((), (), s32[]{:S(2)}) async-start(), calls=%async_computation.4 | async-start | bytes 1327104 | tf_op jit(solution)/shard_map/all_gather | solution.py:121
  61.2 5.1 %copy-start.5 = (bf16[128,512]{1,0:T(8,128)(2,1)S(1)}, bf16[128,512]{1,0:T(8,128)(2,1)}, u32[]{:S(2)}) copy-start(bf16[128,512]{1,0:T(8,128)(2,1)} %param.13) | copy-start | bytes 393220
  61.2 22.9 %all-to-all-start = ((bf16[8,2,23040]{2,1,0:T(2,128)(2,1)}), bf16[8,2,23040]{2,1,0:T(2,128)(2,1)S(1)}, u32[]{:S(2)}, u32[]{:S(2)}) async-start(bf16[8,2,23040]{2,1,0:T(2,128)(2,1)} %reshape.32), calls=%async_computation | async-start | bytes 1474560 | tf_op jit(solution)/shard_map/all_to_all | solution.py:113
  163.5 43.5 %copy-start.2 = (bf16[6,96,128]{2,1,0:T(8,128)(2,1)S(1)}, bf16[6,96,128]{2,1,0:T(8,128)(2,1)}, u32[]{:S(2)}) copy-start(bf16[6,96,128]{2,1,0:T(8,128)(2,1)} %shard_map.91) | copy-start | bytes 442372
  163.5 43.5 %copy-start.3 = (bf16[6,96,128]{2,1,0:T(8,128)(2,1)S(1)}, bf16[6,96,128]{2,1,0:T(8,128)(2,1)}, u32[]{:S(2)}) copy-start(bf16[6,96,128]{2,1,0:T(8,128)(2,1)} %shard_map.92) | copy-start | bytes 442372
  163.5 43.5 %copy-start.4 = (bf16[6,96,128]{2,1,0:T(8,128)(2,1)S(1)}, bf16[6,96,128]{2,1,0:T(8,128)(2,1)}, u32[]{:S(2)}) copy-start(bf16[6,96,128]{2,1,0:T(8,128)(2,1)} %shard_map.93) | copy-start | bytes 442372
Sparse Core Ops, SparseCore 0:
  11.8 47.8 all-gather.4
  61.4 43.9 all-gather.6
  107.2 43.1 all-gather.8
  152.0 41.8 all-gather.10

commit v3 on v2

--- a/solution.py
+++ b/solution.py
@@ -6,9 +6,6 @@
 from jax.experimental import pallas as pl
 from jax.experimental.pallas import tpu as pltpu
 from jax.sharding import PartitionSpec as P
-
-
-CHUNKS = 4
 
 
 def layer_norm(pair_block, norm_gain, norm_shift):
@@ -97,6 +94,96 @@
     )
 
 
+def exchange_kernel(normed_ref, payload_ref, all_ref, bias_ref, norm_send, norm_recv, bias_send, bias_recv, local_sem):
+    col_count = lax.axis_size("cols")
+    row_count = lax.axis_size("rows")
+    group = row_count // col_count
+    me_r = lax.axis_index("rows")
+    me_c = lax.axis_index("cols")
+    width = normed_ref.shape[1]
+    home = pl.ds(pl.multiple_of(me_c * width, width), width)
+    mesh_id = pl.DeviceIdType.MESH
+    copies = []
+    local = pltpu.make_async_copy(normed_ref, all_ref.at[:, home, :], local_sem.at[0])
+    local.start()
+    for p in range(1, col_count):
+        peer = lax.rem(me_c + p, col_count)
+        copy = pltpu.make_async_remote_copy(
+            src_ref=normed_ref,
+            dst_ref=all_ref.at[:, home, :],
+            send_sem=norm_send.at[p],
+            recv_sem=norm_recv,
+            device_id=(me_r, peer),
+            device_id_type=mesh_id,
+        )
+        copy.start()
+        copies.append(copy)
+    target_c = me_r // group
+    slot = me_c * group + lax.rem(me_r, group)
+    self_slot = (target_c == me_c)
+    local_bias = pltpu.make_async_copy(payload_ref, bias_ref.at[slot], bias_recv)
+    bias_copies = []
+    for r in range(row_count):
+        is_self = jnp.logical_and(self_slot, me_r == r)
+        copy = pltpu.make_async_remote_copy(
+            src_ref=payload_ref,
+            dst_ref=bias_ref.at[slot],
+            send_sem=bias_send.at[r],
+            recv_sem=bias_recv,
+            device_id=(r, target_c),
+            device_id_type=mesh_id,
+        )
+
+        @pl.when(jnp.logical_not(is_self))
+        def _():
+            copy.start()
+
+        @pl.when(is_self)
+        def _():
+            local_bias.start()
+
+        bias_copies.append((is_self, copy))
+    local.wait()
+    for copy in copies:
+        copy.wait_send()
+    pltpu.make_async_copy(
+        all_ref.at[:, pl.ds(0, (col_count - 1) * width), :],
+        all_ref.at[:, pl.ds(0, (col_count - 1) * width), :],
+        norm_recv,
+    ).wait()
+    for is_self, copy in bias_copies:
+
+        @pl.when(jnp.logical_not(is_self))
+        def _():
+            copy.wait_send()
+
+    pltpu.make_async_copy(bias_ref, bias_ref, bias_recv).wait()
+
+
+def exchange(normed, payload):
+    row_count, col_count, channels = normed.shape
+    cols = lax.axis_size("cols")
+    rows = lax.axis_size("rows")
+    any_spec = pl.BlockSpec(memory_space=pl.ANY)
+    return pl.pallas_call(
+        exchange_kernel,
+        out_shape=(
+            jax.ShapeDtypeStruct((row_count, cols * col_count, channels), normed.dtype),
+            jax.ShapeDtypeStruct((rows,) + payload.shape, payload.dtype),
+        ),
+        in_specs=[any_spec, any_spec],
+        out_specs=(any_spec, any_spec),
+        scratch_shapes=[
+            pltpu.SemaphoreType.DMA((cols,)),
+            pltpu.SemaphoreType.DMA(()),
+            pltpu.SemaphoreType.DMA((rows,)),
+            pltpu.SemaphoreType.DMA(()),
+            pltpu.SemaphoreType.DMA((1,)),
+        ],
+        compiler_params=pltpu.CompilerParams(has_side_effects=True),
+    )(normed, payload)
+
+
 def shards(
     pair, token_mask, norm_gain, norm_shift, in_weight, gate_bias, bias_weight, out_weight, out_bias
 ):
@@ -109,20 +196,17 @@
         token_mask.astype(jnp.bfloat16)[None, None, :], (1,) + bias_tile.shape[1:]
     )
     payload = jnp.concatenate((bias_tile, mask_tile), axis=0)
-    bias_cols = lax.all_gather(payload, "rows", axis=1, tiled=True)
-    bias = lax.all_to_all(bias_cols, "cols", 1, 2, tiled=True)
+    normed_all, bias_in = exchange(normed, payload)
+    cols = lax.axis_size("cols")
+    group = lax.axis_size("rows") // cols
+    slots, width = payload.shape[0], payload.shape[2]
+    bias = bias_in.reshape(cols, group, slots, payload.shape[1], width)
+    bias = jnp.transpose(bias, (2, 1, 3, 0, 4)).reshape(
+        slots, group * payload.shape[1], cols * width
+    )
     wqg = jnp.concatenate((in_weight[:, :inner], in_weight[:, 3 * inner :]), axis=1)
     wkv = in_weight[:, inner : 3 * inner]
-    row_count = normed.shape[0]
-    chunk = row_count // CHUNKS
-    outs = []
-    for q in range(CHUNKS):
-        part = normed[q * chunk : (q + 1) * chunk]
-        part_all = lax.all_gather(part, "cols", axis=1, tiled=True)
-        outs.append(
-            attend(part, part_all, bias, wqg, wkv, gate_bias, out_weight, out_bias)
-        )
-    return jnp.concatenate(outs, axis=0)
+    return attend(normed, normed_all, bias, wqg, wkv, gate_bias, out_weight, out_bias)
 
 
 def solution(mesh):

time: 216 us -> 163 us (0.75)
  the two profiles are of different devices: /device:TPU:64 before, /device:TPU:91 now
where the time goes in v3:
time: 163 us
  Pallas kernels  153 us (94%)
  other arithmetic  5.38 us (3%)
  local copies, waits for them, and re-layouts  3.95 us (2%)
    pallas_call x1, Pallas kernels, exchange(): pl.pallas_call(exchange_kernel, out_shape=(jax.ShapeDtypeStruct((row_coun...  106 us
    pallas_call x1, Pallas kernels, attend(): pl.pallas_call(functools.partial(attend_kernel, head_count, head_size), o...  46.6 us

profile of v3, /device:TPU:91, one launch (start us, length us, event | category | flops | bytes accessed | tf_op | source)
XLA Modules:
  0.0 162.9 jit_solution(4338390414781016213)
XLA Ops:
  0.0 0.0 copy-start
  0.0 0.0 copy-start.2
  0.0 0.0 copy-start.4
  0.0 0.0 copy-start.5
  0.0 0.0 copy-start.6
  0.0 1.4 convert_reduce_fusion
  1.5 1.9 %fusion.2 = f32[24,96]{1,0:T(8,128)S(1)} fusion(bf16[24,96,128]{2,1,0:T(8,128)(2,1)} %param.9, f32[24,96]{1,0:T(8,128)S(1)} %broadcast_multiply_fusion), kind=kLoop, calls=%fused_computation.4 | loop fusion | flops 1177344 | bytes 608256 | tf_op jit(solution)/shard_map/reduce_sum | solution.py:14
  3.3 0.0 copy-done.2
  3.4 0.0 copy-done.4
  3.4 0.0 copy-done.5
  3.4 0.8 fusion.5.normed_ref.own_ref
  4.2 0.0 copy-done.6
  4.2 0.0 copy-start.1
  4.3 0.0 copy-done
  4.3 0.5 fusion.7
  4.7 0.6 pad_maximum_fusion.1.payload_ref
  5.4 0.0 copy-done.1
  5.4 106.4 %shard_map.91 = (bf16[24,768,128]{2,1,0:T(8,128)(2,1)}, bf16[32,5,24,96]{3,2,1,0:T(8,128)(2,1)}) custom-call(bf16[24,96,128]{2,1,0:T(8,128)(2,1)} %copy-done.1, bf16[5,24,96]{2,1,0:T(8,128)(2,1)} %pad_maximum_fusion.1.payload_ref), custom_call_target="tpu_custom_call" | custom-call | tf_op jit(solution)/shard_map/pallas_call | solution.py:168
  111.8 1.6 copy.16
  113.3 0.0 copy-start.3
  113.4 1.7 %reshape.30.bias_ref = bf16[5,96,768]{2,1,0:T(8,128)(2,1)} reshape(bf16[5,4,24,8,96]{4,3,2,1,0:T(8,128)(2,1)S(1)} %bitcast.15) | data formatting | bytes 1474560 | tf_op jit(solution)/shard_map/reshape | solution.py:204
  115.0 0.0 copy-done.3
  115.0 0.6 pad_maximum_fusion.wqg_ref
  115.7 0.6 slice.11.wkv_ref
  116.3 46.6 %shard_map.92 = bf16[24,96,128]{2,1,0:T(8,128)(2,1)} custom-call(bf16[24,96,128]{2,1,0:T(8,128)(2,1)} %copy-done.1, bf16[24,768,128]{2,1,0:T(8,128)(2,1)} %get-tuple-element.7.all_ref, bf16[5,96,768]{2,1,0:T(8,128)(2,1)} %reshape.30.bias_ref, bf16[128,256]{1,0:T(8,128)(2,1)} %pad_maximum_fusion.wqg_ref, bf16[128,256]{1,0:T(8,128)(2,1)} %slice.11.wkv_ref, ...), custom_call_target="tpu_custom_call" | custom-call | tf_op jit(solution)/shard_map/pallas_call | solution.py:70
  (6 shorter events, 0.0 us)
Async XLA Ops:
  0.0 4.3 %copy-start = (bf16[128,4]{0,1:T(4,128)(2,1)S(1)}, bf16[128,4]{0,1:T(4,128)(2,1)}, u32[]{:S(2)}) copy-start(bf16[128,4]{0,1:T(4,128)(2,1)} %param.15) | copy-start | bytes 3076
  0.0 3.3 %copy-start.2 = (bf16[24,96,128]{2,1,0:T(8,128)(2,1)S(1)}, bf16[24,96,128]{2,1,0:T(8,128)(2,1)}, u32[]{:S(2)}) copy-start(bf16[24,96,128]{2,1,0:T(8,128)(2,1)} %param.9) | copy-start | bytes 1769476
  0.0 3.4 %copy-start.4 = (f32[128]{0:T(128)S(1)}, f32[128]{0:T(128)}, u32[]{:S(2)}) copy-start(f32[128]{0:T(128)} %param.12) | copy-start | bytes 1540
  0.0 3.4 %copy-start.5 = (f32[128]{0:T(128)S(1)}, f32[128]{0:T(128)}, u32[]{:S(2)}) copy-start(f32[128]{0:T(128)} %param.11) | copy-start | bytes 1540
  0.0 4.2 %copy-start.6 = (s32[96]{0:T(128)S(1)}, s32[96]{0:T(128)}, u32[]{:S(2)}) copy-start(s32[96]{0:T(128)} %param.10) | copy-start | bytes 1156
  4.2 1.1 copy-start.1
  113.3 1.7 %copy-start.3 = (bf16[128,512]{1,0:T(8,128)(2,1)S(1)}, bf16[128,512]{1,0:T(8,128)(2,1)}, u32[]{:S(2)}) copy-start(bf16[128,512]{1,0:T(8,128)(2,1)} %param.13) | copy-start | bytes 393220

commit v4 on v2

v4 whole, which is shorter than its diff:
```python
import functools

import jax
import jax.numpy as jnp
from jax import lax
from jax.experimental import pallas as pl
from jax.experimental.pallas import tpu as pltpu
from jax.sharding import PartitionSpec as P


def layer_norm(pair_block, norm_gain, norm_shift):
    as_float = pair_block.astype(jnp.float32)
    center = jnp.mean(as_float, axis=-1, keepdims=True)
    spread = jnp.mean(jnp.square(as_float - center), axis=-1, keepdims=True)
    return ((as_float - center) * lax.rsqrt(spread + 1e-05) * norm_gain + norm_shift).astype(
        jnp.bfloat16
    )


CHUNKS = 4


def row_update(own, row, bias_ref, masking, wqg, wkv, gb, ow, ob, head_count, head_size):
    inner = head_count * head_size
    qg = jnp.dot(own, wqg, preferred_element_type=jnp.float32)
    queries = (qg[:, :inner] * head_size ** (-0.5)).astype(jnp.bfloat16)
    gates = jax.nn.sigmoid(qg[:, inner:] + gb)
    kv = jnp.dot(row, wkv, preferred_element_type=jnp.float32)
    keys = kv[:, :inner].astype(jnp.bfloat16)
    values = kv[:, inner:].astype(jnp.bfloat16)
    lane_head = lax.broadcasted_iota(jnp.int32, (1, inner), 1) // head_size
    attended = jnp.zeros((own.shape[0], inner), jnp.float32)
    for h in range(head_count):
        in_head = lane_head == h
        q_h = jnp.where(in_head, queries, jnp.zeros_like(queries))
        scores = lax.dot_general(
            q_h, keys, (((1,), (1,)), ((), ())), preferred_element_type=jnp.float32
        )
        scores = scores + bias_ref[h]
        scores = scores + masking
        top = jnp.max(scores, axis=-1, keepdims=True)
        expo = jnp.exp(scores - top)
        totals = jnp.sum(expo, axis=-1, keepdims=True)
        mixed = jnp.dot(expo.astype(jnp.bfloat16), values, preferred_element_type=jnp.float32)
        attended = jnp.where(in_head, mixed / totals, attended)
    gated = (gates * attended).astype(jnp.bfloat16)
    return jnp.dot(gated, ow, preferred_element_type=jnp.float32) + ob


def fused_kernel(
    head_count,
    own_ref,
    pay_ref,
    wqg_ref,
    wkv_ref,
    gb_ref,
    ow_ref,
    ob_ref,
    out_ref,
    rows_buf,
    pieces,
    bias_buf,
    norm_send,
    norm_recv,
    local_sem,
    bias_send,
    bias_recv,
):
    col_count = lax.axis_size("cols")
    row_count = lax.axis_size("rows")
    group = row_count // col_count
    me_r = lax.axis_index("rows")
    me_c = lax.axis_index("cols")
    own_rows, width, channels = own_ref.shape
    depth = pay_ref.shape[1]
    chunk = own_rows // CHUNKS
    mesh_id = pl.DeviceIdType.MESH
    target_c = me_r // group
    is_home = target_c == me_c
    barrier = pltpu.get_barrier_semaphore()
    for p in range(1, col_count):
        pl.semaphore_signal(
            barrier, 1, device_id=(me_r, lax.rem(me_c + p, col_count)), device_id_type=mesh_id
        )
    for r in range(row_count):

        @pl.when(jnp.logical_not(jnp.logical_and(is_home, me_r == r)))
        def _():
            pl.semaphore_signal(barrier, 1, device_id=(r, target_c), device_id_type=mesh_id)

    for m in range(group):
        for c in range(col_count):

            @pl.when(jnp.logical_not(jnp.logical_and(group * me_c + m == me_r, me_c == c)))
            def _():
                pl.semaphore_signal(
                    barrier, 1, device_id=(group * me_c + m, c), device_id_type=mesh_id
                )

    pl.semaphore_wait(barrier, col_count - 1 + 2 * (row_count - is_home.astype(jnp.int32)))

    slot = me_c * group + lax.rem(me_r, group)
    local_bias = pltpu.make_async_copy(pay_ref, pieces.at[slot], bias_recv)
    bias_copies = []
    for r in range(row_count):
        is_self = jnp.logical_and(is_home, me_r == r)
        copy = pltpu.make_async_remote_copy(
            src_ref=pay_ref,
            dst_ref=pieces.at[slot],
            send_sem=bias_send.at[r],
            recv_sem=bias_recv,
            device_id=(r, target_c),
            device_id_type=mesh_id,
        )

        @pl.when(jnp.logical_not(is_self))
        def _():
            copy.start()

        @pl.when(is_self)
        def _():
            local_bias.start()

        bias_copies.append((is_self, copy))

    home = pl.ds(pl.multiple_of(me_c * width, width), width)
    norm_copies = []
    locals_ = []
    for q in range(CHUNKS):
        part = pl.ds(q * chunk, chunk)
        local = pltpu.make_async_copy(own_ref.at[part], rows_buf.at[part, home, :], local_sem.at[q])
        local.start()
        locals_.append(local)
        for p in range(1, col_count):
            copy = pltpu.make_async_remote_copy(
                src_ref=own_ref.at[part],
                dst_ref=rows_buf.at[part, home, :],
                send_sem=norm_send.at[q, p],
                recv_sem=norm_recv.at[q],
                device_id=(me_r, lax.rem(me_c + p, col_count)),
                device_id_type=mesh_id,
            )
            copy.start()
            norm_copies.append(copy)

    pltpu.make_async_copy(pieces, pieces, bias_recv).wait()
    for c in range(col_count):
        for m in range(group):
            bias_buf[:, m * depth : (m + 1) * depth, c * width : (c + 1) * width] = pieces[
                c * group + m
            ].astype(jnp.float32)
    masking = 1000000000.0 * (bias_buf[head_count, 0:1, :] - 1.0)
    inner = ow_ref.shape[0]
    head_size = inner // head_count

    for q in range(CHUNKS):
        locals_[q].wait()
        arrived = pl.ds(0, (col_count - 1) * width)
        pltpu.make_async_copy(
            rows_buf.at[pl.ds(q * chunk, chunk), arrived, :],
            rows_buf.at[pl.ds(q * chunk, chunk), arrived, :],
            norm_recv.at[q],
        ).wait()

        def body(i, carry):
            updated = row_update(
                own_ref[i],
                rows_buf[i],
                bias_buf,
                masking,
                wqg_ref[...],
                wkv_ref[...],
                gb_ref[...],
                ow_ref[...],
                ob_ref[...],
                head_count,
                head_size,
            )
            out_ref[i] = updated.astype(out_ref.dtype)
            return carry

        lax.fori_loop(q * chunk, (q + 1) * chunk, body, 0)

    for copy in norm_copies:
        copy.wait_send()
    for is_self, copy in bias_copies:

        @pl.when(jnp.logical_not(is_self))
        def _():
            copy.wait_send()


def fused(normed, payload, wqg, wkv, gate_bias, out_weight, out_bias):
    own_rows, width, channels = normed.shape
    cols = lax.axis_size("cols")
    rows = lax.axis_size("rows")
    slots, depth, _ = payload.shape
    group = rows // cols
    inner = out_weight.shape[0]
    vmem = pl.BlockSpec(memory_space=pltpu.VMEM)
    return pl.pallas_call(
        functools.partial(fused_kernel, slots - 1),
        out_shape=jax.ShapeDtypeStruct(normed.shape, jnp.bfloat16),
        in_specs=[vmem] * 7,
        out_specs=vmem,
        scratch_shapes=[
            pltpu.VMEM((own_rows, cols * width, channels), normed.dtype),
            pltpu.VMEM((rows,) + payload.shape, payload.dtype),
            pltpu.VMEM((slots, group * depth, cols * width), jnp.float32),
            pltpu.SemaphoreType.DMA((CHUNKS, cols)),
            pltpu.SemaphoreType.DMA((CHUNKS,)),
            pltpu.SemaphoreType.DMA((CHUNKS,)),
            pltpu.SemaphoreType.DMA((rows,)),
            pltpu.SemaphoreType.DMA(()),
        ],
        compiler_params=pltpu.CompilerParams(
            has_side_effects=True, collective_id=0, vmem_limit_bytes=48 * 1024 * 1024
        ),
    )(
        normed,
        payload,
        wqg,
        wkv,
        gate_bias.reshape(1, inner),
        out_weight,
        out_bias.reshape(1, channels),
    )


def shards(
    pair, token_mask, norm_gain, norm_shift, in_weight, gate_bias, bias_weight, out_weight, out_bias
):
    inner = out_weight.shape[0]
    normed = layer_norm(pair, norm_gain, norm_shift)
    bias_tile = jnp.einsum(
        "jkc,ch->hjk", normed, bias_weight, preferred_element_type=jnp.float32
    ).astype(jnp.bfloat16)
    mask_tile = jnp.broadcast_to(
        token_mask.astype(jnp.bfloat16)[None, None, :], (1,) + bias_tile.shape[1:]
    )
    payload = jnp.concatenate((bias_tile, mask_tile), axis=0)
    wqg = jnp.concatenate((in_weight[:, :inner], in_weight[:, 3 * inner :]), axis=1)
    wkv = in_weight[:, inner : 3 * inner]
    return fused(normed, payload, wqg, wkv, gate_bias, out_weight, out_bias)


def solution(mesh):
    placed = (P("rows", "cols", None), P("cols"), P(), P(), P(), P(), P(), P(), P())
    return jax.shard_map(
        shards, mesh=mesh, in_specs=placed, out_specs=P("rows", "cols", None), check_vma=False
    )
```

time: 216 us -> 122 us (0.56)
  the two profiles are of different devices: /device:TPU:64 before, /device:TPU:48 now
where the time goes in v4:
time: 122 us
  Pallas kernels  116 us (95%)
  other arithmetic  3.76 us (3%)
    pallas_call x1, Pallas kernels, fused(): pl.pallas_call(functools.partial(fused_kernel, slots - 1), out_shape=jax....  116 us

profile of v4, /device:TPU:48, one launch (start us, length us, event | category | flops | bytes accessed | tf_op | source)
XLA Modules:
  0.0 121.8 jit_solution(8724206006154127451)
XLA Ops:
  0.0 0.0 copy-start
  0.0 0.0 copy-start.4
  0.0 0.7 convert_element_type.19
  0.7 0.0 copy-start.5
  0.7 1.4 %convert_reduce_fusion = f32[24,96]{1,0:T(8,128)S(1)} fusion(bf16[24,96,128]{2,1,0:T(8,128)(2,1)} %param.9), kind=kLoop, calls=%fused_computation.1 | loop fusion | flops 587520 | bytes 599040 | tf_op jit(solution)/shard_map/reduce_sum | solution.py:13
  2.1 0.0 copy-start.6
  2.1 0.0 copy-start.7
  2.2 0.0 copy-done.4
  2.2 0.8 fusion.2
  3.0 0.0 copy-done.5
  3.0 0.0 copy-done.6
  3.1 0.0 copy-done.7
  3.1 0.8 fusion.5.own_ref
  3.9 0.0 copy-done
  3.9 0.0 copy-start.1
  3.9 0.0 copy-start.2
  3.9 0.0 copy-start.3
  3.9 0.5 fusion.7
  4.4 0.2 copy-done.1
  4.7 0.0 copy-done.2
  4.7 0.0 copy-done.3
  4.7 116.3 %shard_map.91 = bf16[24,96,128]{2,1,0:T(8,128)(2,1)S(1)} custom-call(bf16[24,96,128]{2,1,0:T(8,128)(2,1)S(1)} %fusion.5.own_ref, bf16[5,24,96]{2,1,0:T(8,128)(2,1)S(1)} %pad_maximum_fusion.1.pay_ref, bf16[128,256]{1,0:T(8,128)(2,1)S(1)} %pad_maximum_fusion.wqg_ref, bf16[128,256]{1,0:T(8,128)(2,1)S(1)} %slice.11.wkv_ref, f32[1,128]{1,0:T(1,128)S(1)} %bitcast.9, ...), custom_call_target="tpu_custom_call" | custom-call | tf_op jit(solution)/shard_map/pallas_call | solution.py:201
  121.0 0.8 copy.16
  (8 shorter events, 0.1 us)
Async XLA Ops:
  0.0 3.9 %copy-start = (bf16[128,4]{0,1:T(4,128)(2,1)S(1)}, bf16[128,4]{0,1:T(4,128)(2,1)}, u32[]{:S(2)}) copy-start(bf16[128,4]{0,1:T(4,128)(2,1)} %param.15) | copy-start | bytes 3076
  0.0 2.2 %copy-start.4 = (bf16[24,96,128]{2,1,0:T(8,128)(2,1)S(1)}, bf16[24,96,128]{2,1,0:T(8,128)(2,1)}, u32[]{:S(2)}) copy-start(bf16[24,96,128]{2,1,0:T(8,128)(2,1)} %param.9) | copy-start | bytes 1769476
  0.7 2.3 %copy-start.5 = (bf16[128,512]{1,0:T(8,128)(2,1)S(1)}, bf16[128,512]{1,0:T(8,128)(2,1)}, u32[]{:S(2)}) copy-start(bf16[128,512]{1,0:T(8,128)(2,1)} %param.13) | copy-start | bytes 393220
  2.1 0.9 copy-start.6
  2.1 0.9 copy-start.7
  3.9 0.8 copy-start.1
  3.9 0.8 copy-start.2
  3.9 0.7 copy-start.3

commit v5 on v4

--- a/solution.py
+++ b/solution.py
@@ -25,17 +25,16 @@
     qg = jnp.dot(own, wqg, preferred_element_type=jnp.float32)
     queries = (qg[:, :inner] * head_size ** (-0.5)).astype(jnp.bfloat16)
     gates = jax.nn.sigmoid(qg[:, inner:] + gb)
-    kv = jnp.dot(row, wkv, preferred_element_type=jnp.float32)
-    keys = kv[:, :inner].astype(jnp.bfloat16)
-    values = kv[:, inner:].astype(jnp.bfloat16)
+    keys_t = lax.dot_general(
+        wkv[:, :inner], row, (((0,), (1,)), ((), ())), preferred_element_type=jnp.float32
+    ).astype(jnp.bfloat16)
+    values = jnp.dot(row, wkv[:, inner:], preferred_element_type=jnp.float32).astype(jnp.bfloat16)
     lane_head = lax.broadcasted_iota(jnp.int32, (1, inner), 1) // head_size
     attended = jnp.zeros((own.shape[0], inner), jnp.float32)
     for h in range(head_count):
         in_head = lane_head == h
         q_h = jnp.where(in_head, queries, jnp.zeros_like(queries))
-        scores = lax.dot_general(
-            q_h, keys, (((1,), (1,)), ((), ())), preferred_element_type=jnp.float32
-        )
+        scores = jnp.dot(q_h, keys_t, preferred_element_type=jnp.float32)
         scores = scores + bias_ref[h]
         scores = scores + masking
         top = jnp.max(scores, axis=-1, keepdims=True)

time: 122 us -> 121 us (level)
  no operation moved by 1% of the time
where the time goes in v5:
time: 121 us
  Pallas kernels  115 us (95%)
  other arithmetic  3.76 us (3%)
    pallas_call x1, Pallas kernels, fused(): pl.pallas_call(functools.partial(fused_kernel, slots - 1), out_shape=jax....  115 us

profile of v5, /device:TPU:48, one launch (start us, length us, event | category | flops | bytes accessed | tf_op | source)
XLA Modules:
  0.0 120.8 jit_solution(2166164641124809399)
XLA Ops:
  0.0 0.0 copy-start
  0.0 0.0 copy-start.4
  0.0 0.7 convert_element_type.19
  0.7 0.0 copy-start.5
  0.7 1.4 %convert_reduce_fusion = f32[24,96]{1,0:T(8,128)S(1)} fusion(bf16[24,96,128]{2,1,0:T(8,128)(2,1)} %param.9), kind=kLoop, calls=%fused_computation.1 | loop fusion | flops 587520 | bytes 599040 | tf_op jit(solution)/shard_map/reduce_sum | solution.py:13
  2.1 0.0 copy-start.6
  2.1 0.0 copy-start.7
  2.2 0.0 copy-done.4
  2.2 0.8 fusion.2
  3.0 0.0 copy-done.5
  3.0 0.0 copy-done.6
  3.1 0.0 copy-done.7
  3.1 0.8 fusion.5.own_ref
  3.9 0.0 copy-done
  3.9 0.0 copy-start.1
  3.9 0.0 copy-start.2
  3.9 0.0 copy-start.3
  3.9 0.5 fusion.7
  4.4 0.2 copy-done.1
  4.7 0.0 copy-done.2
  4.7 0.0 copy-done.3
  4.7 115.3 %shard_map.91 = bf16[24,96,128]{2,1,0:T(8,128)(2,1)S(1)} custom-call(bf16[24,96,128]{2,1,0:T(8,128)(2,1)S(1)} %fusion.5.own_ref, bf16[5,24,96]{2,1,0:T(8,128)(2,1)S(1)} %pad_maximum_fusion.1.pay_ref, bf16[128,256]{1,0:T(8,128)(2,1)S(1)} %pad_maximum_fusion.wqg_ref, bf16[128,256]{1,0:T(8,128)(2,1)S(1)} %slice.11.wkv_ref, f32[1,128]{1,0:T(1,128)S(1)} %bitcast.9, ...), custom_call_target="tpu_custom_call" | custom-call | tf_op jit(solution)/shard_map/pallas_call | solution.py:200
  119.9 0.8 copy.16
  (8 shorter events, 0.1 us)
Async XLA Ops:
  0.0 3.9 %copy-start = (bf16[128,4]{0,1:T(4,128)(2,1)S(1)}, bf16[128,4]{0,1:T(4,128)(2,1)}, u32[]{:S(2)}) copy-start(bf16[128,4]{0,1:T(4,128)(2,1)} %param.15) | copy-start | bytes 3076
  0.0 2.2 %copy-start.4 = (bf16[24,96,128]{2,1,0:T(8,128)(2,1)S(1)}, bf16[24,96,128]{2,1,0:T(8,128)(2,1)}, u32[]{:S(2)}) copy-start(bf16[24,96,128]{2,1,0:T(8,128)(2,1)} %param.9) | copy-start | bytes 1769476
  0.7 2.3 %copy-start.5 = (bf16[128,512]{1,0:T(8,128)(2,1)S(1)}, bf16[128,512]{1,0:T(8,128)(2,1)}, u32[]{:S(2)}) copy-start(bf16[128,512]{1,0:T(8,128)(2,1)} %param.13) | copy-start | bytes 393220
  2.1 0.9 copy-start.6
  2.1 0.9 copy-start.7
  3.9 0.8 copy-start.1
  3.9 0.8 copy-start.2
  3.9 0.7 copy-start.3

commit v6 on v5

--- a/solution.py
+++ b/solution.py
@@ -64,6 +64,7 @@
     local_sem,
     bias_send,
     bias_recv,
+    fwd_sem,
 ):
     col_count = lax.axis_size("cols")
     row_count = lax.axis_size("rows")
@@ -76,37 +77,43 @@
     mesh_id = pl.DeviceIdType.MESH
     target_c = me_r // group
     is_home = target_c == me_c
+    parity = lax.rem(me_r, 2)
+    half = row_count // 2
+    sibling = me_r + 1 - 2 * parity
     barrier = pltpu.get_barrier_semaphore()
     for p in range(1, col_count):
         pl.semaphore_signal(
             barrier, 1, device_id=(me_r, lax.rem(me_c + p, col_count)), device_id_type=mesh_id
         )
-    for r in range(row_count):
+    pl.semaphore_signal(barrier, 1, device_id=(sibling, me_c), device_id_type=mesh_id)
+    for t in range(half):
+        r = 2 * t + parity
 
         @pl.when(jnp.logical_not(jnp.logical_and(is_home, me_r == r)))
         def _():
             pl.semaphore_signal(barrier, 1, device_id=(r, target_c), device_id_type=mesh_id)
 
-    for m in range(group):
+    for u in range(group // 2):
         for c in range(col_count):
-
-            @pl.when(jnp.logical_not(jnp.logical_and(group * me_c + m == me_r, me_c == c)))
+            source = group * me_c + 2 * u + parity
+
+            @pl.when(jnp.logical_not(jnp.logical_and(source == me_r, me_c == c)))
             def _():
-                pl.semaphore_signal(
-                    barrier, 1, device_id=(group * me_c + m, c), device_id_type=mesh_id
-                )
-
-    pl.semaphore_wait(barrier, col_count - 1 + 2 * (row_count - is_home.astype(jnp.int32)))
-
-    slot = me_c * group + lax.rem(me_r, group)
+                pl.semaphore_signal(barrier, 1, device_id=(source, c), device_id_type=mesh_id)
+
+    pl.semaphore_wait(barrier, col_count + 2 * (half - is_home.astype(jnp.int32)))
+
+    block = lax.rem(me_r, group)
+    slot = lax.rem(block, 2) * half + (block // 2) * col_count + me_c
     local_bias = pltpu.make_async_copy(pay_ref, pieces.at[slot], bias_recv)
     bias_copies = []
-    for r in range(row_count):
+    for t in range(half):
+        r = 2 * t + parity
         is_self = jnp.logical_and(is_home, me_r == r)
         copy = pltpu.make_async_remote_copy(
             src_ref=pay_ref,
             dst_ref=pieces.at[slot],
-            send_sem=bias_send.at[r],
+            send_sem=bias_send.at[t],
             recv_sem=bias_recv,
             device_id=(r, target_c),
             device_id_type=mesh_id,
@@ -142,11 +149,22 @@
             copy.start()
             norm_copies.append(copy)
 
-    pltpu.make_async_copy(pieces, pieces, bias_recv).wait()
+    direct = pieces.at[pl.ds(pl.multiple_of(parity * half, half), half)]
+    pltpu.make_async_copy(direct, direct, bias_recv).wait()
+    forward = pltpu.make_async_remote_copy(
+        src_ref=direct,
+        dst_ref=direct,
+        send_sem=fwd_sem.at[0],
+        recv_sem=fwd_sem.at[1],
+        device_id=(sibling, me_c),
+        device_id_type=mesh_id,
+    )
+    forward.start()
+    forward.wait()
     for c in range(col_count):
         for m in range(group):
             bias_buf[:, m * depth : (m + 1) * depth, c * width : (c + 1) * width] = pieces[
-                c * group + m
+                (m % 2) * half + (m // 2) * col_count + c
             ].astype(jnp.float32)
     masking = 1000000000.0 * (bias_buf[head_count, 0:1, :] - 1.0)
     inner = ow_ref.shape[0]
@@ -209,8 +227,9 @@
             pltpu.SemaphoreType.DMA((CHUNKS, cols)),
             pltpu.SemaphoreType.DMA((CHUNKS,)),
             pltpu.SemaphoreType.DMA((CHUNKS,)),
-            pltpu.SemaphoreType.DMA((rows,)),
+            pltpu.SemaphoreType.DMA((rows // 2,)),
             pltpu.SemaphoreType.DMA(()),
+            pltpu.SemaphoreType.DMA((2,)),
         ],
         compiler_params=pltpu.CompilerParams(
             has_side_effects=True, collective_id=0, vmem_limit_bytes=48 * 1024 * 1024

time: 121 us -> 93.6 us (0.77)
  the two profiles are of different devices: /device:TPU:48 before, /device:TPU:64 now
where the time goes in v6:
time: 93.6 us; the launch traced here: 93.4 us
  Pallas kernels  87.9 us (94%)
  other arithmetic  3.76 us (4%)
  local copies, waits for them, and re-layouts  1.12 us (1%)
    pallas_call x1, Pallas kernels, fused(): pl.pallas_call(functools.partial(fused_kernel, slots - 1), out_shape=jax....  87.9 us

profile of v6, /device:TPU:64, one launch (start us, length us, event | category | flops | bytes accessed | tf_op | source)
XLA Modules:
  0.0 93.4 jit_solution(14552795272750185831)
XLA Ops:
  0.0 0.0 copy-start
  0.0 0.0 copy-start.4
  0.0 0.7 convert_element_type.19
  0.7 0.0 copy-start.5
  0.7 1.4 %convert_reduce_fusion = f32[24,96]{1,0:T(8,128)S(1)} fusion(bf16[24,96,128]{2,1,0:T(8,128)(2,1)} %param.9), kind=kLoop, calls=%fused_computation.1 | loop fusion | flops 587520 | bytes 599040 | tf_op jit(solution)/shard_map/reduce_sum | solution.py:13
  2.1 0.0 copy-start.6
  2.1 0.0 copy-start.7
  2.2 0.0 copy-done.4
  2.2 0.8 fusion.2
  3.0 0.0 copy-done.5
  3.0 0.0 copy-done.6
  3.1 0.0 copy-done.7
  3.1 0.8 fusion.5.own_ref
  3.9 0.0 copy-done
  3.9 0.0 copy-start.1
  3.9 0.0 copy-start.2
  3.9 0.0 copy-start.3
  3.9 0.5 fusion.7
  4.4 0.2 copy-done.1
  4.7 0.0 copy-done.2
  4.7 0.0 copy-done.3
  4.7 87.9 %shard_map.91 = bf16[24,96,128]{2,1,0:T(8,128)(2,1)S(1)} custom-call(bf16[24,96,128]{2,1,0:T(8,128)(2,1)S(1)} %fusion.5.own_ref, bf16[5,24,96]{2,1,0:T(8,128)(2,1)S(1)} %pad_maximum_fusion.1.pay_ref, bf16[128,256]{1,0:T(8,128)(2,1)S(1)} %pad_maximum_fusion.wqg_ref, bf16[128,256]{1,0:T(8,128)(2,1)S(1)} %slice.11.wkv_ref, f32[1,128]{1,0:T(1,128)S(1)} %bitcast.9, ...), custom_call_target="tpu_custom_call" | custom-call | tf_op jit(solution)/shard_map/pallas_call | solution.py:218
  92.6 0.8 copy.16
  (8 shorter events, 0.1 us)
Async XLA Ops:
  0.0 3.9 %copy-start = (bf16[128,4]{0,1:T(4,128)(2,1)S(1)}, bf16[128,4]{0,1:T(4,128)(2,1)}, u32[]{:S(2)}) copy-start(bf16[128,4]{0,1:T(4,128)(2,1)} %param.15) | copy-start | bytes 3076
  0.0 2.2 %copy-start.4 = (bf16[24,96,128]{2,1,0:T(8,128)(2,1)S(1)}, bf16[24,96,128]{2,1,0:T(8,128)(2,1)}, u32[]{:S(2)}) copy-start(bf16[24,96,128]{2,1,0:T(8,128)(2,1)} %param.9) | copy-start | bytes 1769476
  0.7 2.3 %copy-start.5 = (bf16[128,512]{1,0:T(8,128)(2,1)S(1)}, bf16[128,512]{1,0:T(8,128)(2,1)}, u32[]{:S(2)}) copy-start(bf16[128,512]{1,0:T(8,128)(2,1)} %param.13) | copy-start | bytes 393220
  2.1 0.9 copy-start.6
  2.1 0.9 copy-start.7
  3.9 0.8 copy-start.1
  3.9 0.8 copy-start.2
  3.9 0.7 copy-start.3

commit v7 on v6

--- a/solution.py
+++ b/solution.py
@@ -72,7 +72,7 @@
     me_r = lax.axis_index("rows")
     me_c = lax.axis_index("cols")
     own_rows, width, channels = own_ref.shape
-    depth = pay_ref.shape[1]
+    depth = pay_ref.shape[0] - 1
     chunk = own_rows // CHUNKS
     mesh_id = pl.DeviceIdType.MESH
     target_c = me_r // group
@@ -163,9 +163,15 @@
     forward.wait()
     for c in range(col_count):
         for m in range(group):
-            bias_buf[:, m * depth : (m + 1) * depth, c * width : (c + 1) * width] = pieces[
-                (m % 2) * half + (m // 2) * col_count + c
-            ].astype(jnp.float32)
+            piece = pieces[(m % 2) * half + (m // 2) * col_count + c].astype(jnp.float32)
+            for h in range(head_count):
+                bias_buf[h, m * depth : (m + 1) * depth, c * width : (c + 1) * width] = piece[
+                    :depth, h * width : (h + 1) * width
+                ]
+            if m == 0:
+                bias_buf[head_count, 0:1, c * width : (c + 1) * width] = piece[
+                    depth : depth + 1, 0:width
+                ]
     masking = 1000000000.0 * (bias_buf[head_count, 0:1, :] - 1.0)
     inner = ow_ref.shape[0]
     head_size = inner // head_count
@@ -207,16 +213,17 @@
             copy.wait_send()
 
 
-def fused(normed, payload, wqg, wkv, gate_bias, out_weight, out_bias):
+def fused(normed, payload, wqg, wkv, gate_bias, out_weight, out_bias, head_count):
     own_rows, width, channels = normed.shape
     cols = lax.axis_size("cols")
     rows = lax.axis_size("rows")
-    slots, depth, _ = payload.shape
+    slots = head_count + 1
+    depth = payload.shape[0] - 1
     group = rows // cols
     inner = out_weight.shape[0]
     vmem = pl.BlockSpec(memory_space=pltpu.VMEM)
     return pl.pallas_call(
-        functools.partial(fused_kernel, slots - 1),
+        functools.partial(fused_kernel, head_count),
         out_shape=jax.ShapeDtypeStruct(normed.shape, jnp.bfloat16),
         in_specs=[vmem] * 7,
         out_specs=vmem,
@@ -250,16 +257,18 @@
 ):
     inner = out_weight.shape[0]
     normed = layer_norm(pair, norm_gain, norm_shift)
+    rows, width, _ = normed.shape
+    head_count = bias_weight.shape[1]
     bias_tile = jnp.einsum(
-        "jkc,ch->hjk", normed, bias_weight, preferred_element_type=jnp.float32
+        "jkc,ch->jhk", normed, bias_weight, preferred_element_type=jnp.float32
     ).astype(jnp.bfloat16)
-    mask_tile = jnp.broadcast_to(
-        token_mask.astype(jnp.bfloat16)[None, None, :], (1,) + bias_tile.shape[1:]
-    )
-    payload = jnp.concatenate((bias_tile, mask_tile), axis=0)
+    mask_row = jnp.tile(token_mask.astype(jnp.bfloat16), head_count)
+    payload = jnp.concatenate(
+        (bias_tile.reshape(rows, head_count * width), mask_row[None, :]), axis=0
+    )
     wqg = jnp.concatenate((in_weight[:, :inner], in_weight[:, 3 * inner :]), axis=1)
     wkv = in_weight[:, inner : 3 * inner]
-    return fused(normed, payload, wqg, wkv, gate_bias, out_weight, out_bias)
+    return fused(normed, payload, wqg, wkv, gate_bias, out_weight, out_bias, head_count)
 
 
 def solution(mesh):

time: 93.6 us -> 91.1 us (0.973)
  Pallas kernels: 87.9 us -> 84.5 us
    pallas_call x1, Pallas kernels: 87.9 us -> 84.5 us  [fused(): pl.pallas_call(functools.partial(fused_kernel, head_count), out_shape=jax...]
where the time goes in v7:
time: 91.1 us; the launch traced here: 90.1 us
  Pallas kernels  84.5 us (93%)
  other arithmetic  3.76 us (4%)
  local copies, waits for them, and re-layouts  1.21 us (1%)
    pallas_call x1, Pallas kernels, fused(): pl.pallas_call(functools.partial(fused_kernel, head_count), out_shape=jax...  84.5 us

profile of v7, /device:TPU:64, one launch (start us, length us, event | category | flops | bytes accessed | tf_op | source)
XLA Modules:
  0.0 90.1 jit_solution(4644231255668349030)
XLA Ops:
  0.0 0.0 copy-start
  0.0 0.0 copy-start.4
  0.0 0.7 convert_element_type.19
  0.7 0.1 broadcast_in_dim_tile.3
  0.8 0.0 copy-start.5
  0.8 1.4 %convert_reduce_fusion = f32[24,96]{1,0:T(8,128)S(1)} fusion(bf16[24,96,128]{2,1,0:T(8,128)(2,1)} %param.9), kind=kLoop, calls=%fused_computation.1 | loop fusion | flops 587520 | bytes 599040 | tf_op jit(solution)/shard_map/reduce_sum | solution.py:13
  2.2 0.0 copy-start.6
  2.2 0.0 copy-start.7
  2.2 0.0 copy-done.4
  2.3 0.8 fusion.2
  3.1 0.0 copy-done.5
  3.1 0.0 copy-done.6
  3.1 0.0 copy-done.7
  3.2 0.8 fusion.5.own_ref
  4.0 0.0 copy-done
  4.0 0.0 copy-start.1
  4.0 0.0 copy-start.2
  4.0 0.0 copy-start.3
  4.0 0.5 fusion.6
  4.5 0.1 reshape.24
  4.6 0.1 copy-done.1
  4.8 0.0 copy-done.2
  4.8 0.0 copy-done.3
  4.8 84.5 %shard_map.91 = bf16[24,96,128]{2,1,0:T(8,128)(2,1)S(1)} custom-call(bf16[24,96,128]{2,1,0:T(8,128)(2,1)S(1)} %fusion.5.own_ref, bf16[25,384]{1,0:T(8,128)(2,1)S(1)} %pad_maximum_fusion.1.pay_ref, bf16[128,256]{1,0:T(8,128)(2,1)S(1)} %pad_maximum_fusion.wqg_ref, bf16[128,256]{1,0:T(8,128)(2,1)S(1)} %slice.11.wkv_ref, f32[1,128]{1,0:T(1,128)S(1)} %bitcast.8, ...), custom_call_target="tpu_custom_call" | custom-call | tf_op jit(solution)/shard_map/pallas_call | solution.py:225
  89.3 0.8 copy.11
  (7 shorter events, 0.0 us)
Async XLA Ops:
  0.0 4.0 %copy-start = (bf16[128,4]{0,1:T(4,128)(2,1)S(1)}, bf16[128,4]{0,1:T(4,128)(2,1)}, u32[]{:S(2)}) copy-start(bf16[128,4]{0,1:T(4,128)(2,1)} %param.15) | copy-start | bytes 3076
  0.0 2.2 %copy-start.4 = (bf16[24,96,128]{2,1,0:T(8,128)(2,1)S(1)}, bf16[24,96,128]{2,1,0:T(8,128)(2,1)}, u32[]{:S(2)}) copy-start(bf16[24,96,128]{2,1,0:T(8,128)(2,1)} %param.9) | copy-start | bytes 1769476
  0.8 2.3 %copy-start.5 = (bf16[128,512]{1,0:T(8,128)(2,1)S(1)}, bf16[128,512]{1,0:T(8,128)(2,1)}, u32[]{:S(2)}) copy-start(bf16[128,512]{1,0:T(8,128)(2,1)} %param.13) | copy-start | bytes 393220
  2.2 0.9 %copy-start.6 = (f32[128]{0:T(128)S(1)}, f32[128]{0:T(128)}, u32[]{:S(2)}) copy-start(f32[128]{0:T(128)} %param.12) | copy-start | bytes 1540
  2.2 0.9 %copy-start.7 = (f32[128]{0:T(128)S(1)}, f32[128]{0:T(128)}, u32[]{:S(2)}) copy-start(f32[128]{0:T(128)} %param.11) | copy-start | bytes 1540
  4.0 0.8 copy-start.1
  4.0 0.8 copy-start.2
  4.0 0.7 copy-start.3

commit v8 on v7

--- a/solution.py
+++ b/solution.py
@@ -17,7 +17,7 @@
     )
 
 
-CHUNKS = 4
+CHUNKS = 8
 
 
 def row_update(own, row, bias_ref, masking, wqg, wkv, gb, ow, ob, head_count, head_size):

time: 91.1 us -> 87.8 us (0.964)
  Pallas kernels: 84.5 us -> 82 us
    pallas_call x1, Pallas kernels: 84.5 us -> 82 us  [fused(): pl.pallas_call(functools.partial(fused_kernel, head_count), out_shape=jax...]
where the time goes in v8:
time: 87.8 us; the launch traced here: 87.6 us
  Pallas kernels  82 us (93%)
  other arithmetic  3.76 us (4%)
  local copies, waits for them, and re-layouts  1.21 us (1%)
    pallas_call x1, Pallas kernels, fused(): pl.pallas_call(functools.partial(fused_kernel, head_count), out_shape=jax...  82 us

profile of v8, /device:TPU:64, one launch (start us, length us, event | category | flops | bytes accessed | tf_op | source)
XLA Modules:
  0.0 87.6 jit_solution(10423671420474941091)
XLA Ops:
  0.0 0.0 copy-start
  0.0 0.0 copy-start.4
  0.0 0.7 convert_element_type.19
  0.7 0.1 broadcast_in_dim_tile.3
  0.8 0.0 copy-start.5
  0.8 1.4 %convert_reduce_fusion = f32[24,96]{1,0:T(8,128)S(1)} fusion(bf16[24,96,128]{2,1,0:T(8,128)(2,1)} %param.9), kind=kLoop, calls=%fused_computation.1 | loop fusion | flops 587520 | bytes 599040 | tf_op jit(solution)/shard_map/reduce_sum | solution.py:13
  2.2 0.0 copy-start.6
  2.2 0.0 copy-start.7
  2.2 0.0 copy-done.4
  2.3 0.8 fusion.2
  3.1 0.0 copy-done.5
  3.1 0.0 copy-done.6
  3.1 0.0 copy-done.7
  3.2 0.8 fusion.5.own_ref
  4.0 0.0 copy-done
  4.0 0.0 copy-start.1
  4.0 0.0 copy-start.2
  4.0 0.0 copy-start.3
  4.0 0.5 fusion.6
  4.5 0.1 reshape.24
  4.6 0.1 copy-done.1
  4.8 0.0 copy-done.2
  4.8 0.0 copy-done.3
  4.8 82.0 %shard_map.91 = bf16[24,96,128]{2,1,0:T(8,128)(2,1)S(1)} custom-call(bf16[24,96,128]{2,1,0:T(8,128)(2,1)S(1)} %fusion.5.own_ref, bf16[25,384]{1,0:T(8,128)(2,1)S(1)} %pad_maximum_fusion.1.pay_ref, bf16[128,256]{1,0:T(8,128)(2,1)S(1)} %pad_maximum_fusion.wqg_ref, bf16[128,256]{1,0:T(8,128)(2,1)S(1)} %slice.11.wkv_ref, f32[1,128]{1,0:T(1,128)S(1)} %bitcast.8, ...), custom_call_target="tpu_custom_call" | custom-call | tf_op jit(solution)/shard_map/pallas_call | solution.py:225
  86.8 0.8 copy.11
  (7 shorter events, 0.0 us)
Async XLA Ops:
  0.0 4.0 %copy-start = (bf16[128,4]{0,1:T(4,128)(2,1)S(1)}, bf16[128,4]{0,1:T(4,128)(2,1)}, u32[]{:S(2)}) copy-start(bf16[128,4]{0,1:T(4,128)(2,1)} %param.15) | copy-start | bytes 3076
  0.0 2.2 %copy-start.4 = (bf16[24,96,128]{2,1,0:T(8,128)(2,1)S(1)}, bf16[24,96,128]{2,1,0:T(8,128)(2,1)}, u32[]{:S(2)}) copy-start(bf16[24,96,128]{2,1,0:T(8,128)(2,1)} %param.9) | copy-start | bytes 1769476
  0.8 2.3 %copy-start.5 = (bf16[128,512]{1,0:T(8,128)(2,1)S(1)}, bf16[128,512]{1,0:T(8,128)(2,1)}, u32[]{:S(2)}) copy-start(bf16[128,512]{1,0:T(8,128)(2,1)} %param.13) | copy-start | bytes 393220
  2.2 0.9 %copy-start.6 = (f32[128]{0:T(128)S(1)}, f32[128]{0:T(128)}, u32[]{:S(2)}) copy-start(f32[128]{0:T(128)} %param.12) | copy-start | bytes 1540
  2.2 0.9 %copy-start.7 = (f32[128]{0:T(128)S(1)}, f32[128]{0:T(128)}, u32[]{:S(2)}) copy-start(f32[128]{0:T(128)} %param.11) | copy-start | bytes 1540
  4.0 0.8 copy-start.1
  4.0 0.8 copy-start.2
  4.0 0.7 copy-start.3

commit v9 on v8

--- a/solution.py
+++ b/solution.py
@@ -30,18 +30,22 @@
     ).astype(jnp.bfloat16)
     values = jnp.dot(row, wkv[:, inner:], preferred_element_type=jnp.float32).astype(jnp.bfloat16)
     lane_head = lax.broadcasted_iota(jnp.int32, (1, inner), 1) // head_size
-    attended = jnp.zeros((own.shape[0], inner), jnp.float32)
+    queries_rows = own.shape[0]
+    stacked = jnp.concatenate(
+        [jnp.where(lane_head == h, queries, jnp.zeros_like(queries)) for h in range(head_count)],
+        axis=0,
+    )
+    scores = jnp.dot(stacked, keys_t, preferred_element_type=jnp.float32)
+    scores = scores + bias_ref[0:head_count].reshape(head_count * queries_rows, -1)
+    scores = scores + masking
+    top = jnp.max(scores, axis=-1, keepdims=True)
+    expo = jnp.exp(scores - top)
+    totals = jnp.sum(expo, axis=-1, keepdims=True)
+    mixed = jnp.dot(expo.astype(jnp.bfloat16), values, preferred_element_type=jnp.float32)
+    attended = jnp.zeros((queries_rows, inner), jnp.float32)
     for h in range(head_count):
-        in_head = lane_head == h
-        q_h = jnp.where(in_head, queries, jnp.zeros_like(queries))
-        scores = jnp.dot(q_h, keys_t, preferred_element_type=jnp.float32)
-        scores = scores + bias_ref[h]
-        scores = scores + masking
-        top = jnp.max(scores, axis=-1, keepdims=True)
-        expo = jnp.exp(scores - top)
-        totals = jnp.sum(expo, axis=-1, keepdims=True)
-        mixed = jnp.dot(expo.astype(jnp.bfloat16), values, preferred_element_type=jnp.float32)
-        attended = jnp.where(in_head, mixed / totals, attended)
+        rows_h = slice(h * queries_rows, (h + 1) * queries_rows)
+        attended = jnp.where(lane_head == h, mixed[rows_h] / totals[rows_h], attended)
     gated = (gates * attended).astype(jnp.bfloat16)
     return jnp.dot(gated, ow, preferred_element_type=jnp.float32) + ob
 

time: 87.8 us -> 84.9 us (0.967)
  Pallas kernels: 82 us -> 79.1 us
    pallas_call x1, Pallas kernels: 82 us -> 79.1 us  [fused(): pl.pallas_call(functools.partial(fused_kernel, head_count), out_shape=jax...]
where the time goes in v9:
time: 84.9 us; the launch traced here: 84.7 us
  Pallas kernels  79.1 us (93%)
  other arithmetic  3.76 us (4%)
  local copies, waits for them, and re-layouts  1.21 us (1%)
    pallas_call x1, Pallas kernels, fused(): pl.pallas_call(functools.partial(fused_kernel, head_count), out_shape=jax...  79.1 us

profile of v9, /device:TPU:64, one launch (start us, length us, event | category | flops | bytes accessed | tf_op | source)
XLA Modules:
  0.0 84.7 jit_solution(7195010103554474926)
XLA Ops:
  0.0 0.0 copy-start
  0.0 0.0 copy-start.4
  0.0 0.7 convert_element_type.19
  0.7 0.1 broadcast_in_dim_tile.3
  0.8 0.0 copy-start.5
  0.8 1.4 %convert_reduce_fusion = f32[24,96]{1,0:T(8,128)S(1)} fusion(bf16[24,96,128]{2,1,0:T(8,128)(2,1)} %param.9), kind=kLoop, calls=%fused_computation.1 | loop fusion | flops 587520 | bytes 599040 | tf_op jit(solution)/shard_map/reduce_sum | solution.py:13
  2.2 0.0 copy-start.6
  2.2 0.0 copy-start.7
  2.2 0.0 copy-done.4
  2.3 0.8 fusion.2
  3.1 0.0 copy-done.5
  3.1 0.0 copy-done.6
  3.1 0.0 copy-done.7
  3.2 0.8 fusion.5.own_ref
  4.0 0.0 copy-done
  4.0 0.0 copy-start.1
  4.0 0.0 copy-start.2
  4.0 0.0 copy-start.3
  4.0 0.5 fusion.6
  4.5 0.1 reshape.24
  4.6 0.1 copy-done.1
  4.8 0.0 copy-done.2
  4.8 0.0 copy-done.3
  4.8 79.1 %shard_map.91 = bf16[24,96,128]{2,1,0:T(8,128)(2,1)S(1)} custom-call(bf16[24,96,128]{2,1,0:T(8,128)(2,1)S(1)} %fusion.5.own_ref, bf16[25,384]{1,0:T(8,128)(2,1)S(1)} %pad_maximum_fusion.1.pay_ref, bf16[128,256]{1,0:T(8,128)(2,1)S(1)} %pad_maximum_fusion.wqg_ref, bf16[128,256]{1,0:T(8,128)(2,1)S(1)} %slice.11.wkv_ref, f32[1,128]{1,0:T(1,128)S(1)} %bitcast.8, ...), custom_call_target="tpu_custom_call" | custom-call | tf_op jit(solution)/shard_map/pallas_call | solution.py:229
  83.9 0.8 copy.11
  (7 shorter events, 0.0 us)
Async XLA Ops:
  0.0 4.0 %copy-start = (bf16[128,4]{0,1:T(4,128)(2,1)S(1)}, bf16[128,4]{0,1:T(4,128)(2,1)}, u32[]{:S(2)}) copy-start(bf16[128,4]{0,1:T(4,128)(2,1)} %param.15) | copy-start | bytes 3076
  0.0 2.2 %copy-start.4 = (bf16[24,96,128]{2,1,0:T(8,128)(2,1)S(1)}, bf16[24,96,128]{2,1,0:T(8,128)(2,1)}, u32[]{:S(2)}) copy-start(bf16[24,96,128]{2,1,0:T(8,128)(2,1)} %param.9) | copy-start | bytes 1769476
  0.8 2.3 %copy-start.5 = (bf16[128,512]{1,0:T(8,128)(2,1)S(1)}, bf16[128,512]{1,0:T(8,128)(2,1)}, u32[]{:S(2)}) copy-start(bf16[128,512]{1,0:T(8,128)(2,1)} %param.13) | copy-start | bytes 393220
  2.2 0.9 %copy-start.6 = (f32[128]{0:T(128)S(1)}, f32[128]{0:T(128)}, u32[]{:S(2)}) copy-start(f32[128]{0:T(128)} %param.12) | copy-start | bytes 1540
  2.2 0.9 %copy-start.7 = (f32[128]{0:T(128)S(1)}, f32[128]{0:T(128)}, u32[]{:S(2)}) copy-start(f32[128]{0:T(128)} %param.11) | copy-start | bytes 1540
  4.0 0.8 copy-start.1
  4.0 0.8 copy-start.2
  4.0 0.7 copy-start.3

commit v10 on v9

--- a/solution.py
+++ b/solution.py
@@ -206,7 +206,7 @@
             out_ref[i] = updated.astype(out_ref.dtype)
             return carry
 
-        lax.fori_loop(q * chunk, (q + 1) * chunk, body, 0)
+        lax.fori_loop(q * chunk, (q + 1) * chunk, body, 0, unroll=True)
 
     for copy in norm_copies:
         copy.wait_send()

time: 84.9 us -> 84.1 us (level)
  no operation moved by 1% of the time
where the time goes in v10:
time: 84.1 us; the launch traced here: 83.9 us
  Pallas kernels  78.3 us (93%)
  other arithmetic  3.76 us (4%)
  local copies, waits for them, and re-layouts  1.21 us (1%)
    pallas_call x1, Pallas kernels, fused(): pl.pallas_call(functools.partial(fused_kernel, head_count), out_shape=jax...  78.3 us

profile of v10, /device:TPU:64, one launch (start us, length us, event | category | flops | bytes accessed | tf_op | source)
XLA Modules:
  0.0 83.9 jit_solution(15942493777969865660)
XLA Ops:
  0.0 0.0 copy-start
  0.0 0.0 copy-start.4
  0.0 0.7 convert_element_type.19
  0.7 0.1 broadcast_in_dim_tile.3
  0.8 0.0 copy-start.5
  0.8 1.4 %convert_reduce_fusion = f32[24,96]{1,0:T(8,128)S(1)} fusion(bf16[24,96,128]{2,1,0:T(8,128)(2,1)} %param.9), kind=kLoop, calls=%fused_computation.1 | loop fusion | flops 587520 | bytes 599040 | tf_op jit(solution)/shard_map/reduce_sum | solution.py:13
  2.2 0.0 copy-start.6
  2.2 0.0 copy-start.7
  2.2 0.0 copy-done.4
  2.3 0.8 fusion.2
  3.1 0.0 copy-done.5
  3.1 0.0 copy-done.6
  3.1 0.0 copy-done.7
  3.2 0.8 fusion.5.own_ref
  4.0 0.0 copy-done
  4.0 0.0 copy-start.1
  4.0 0.0 copy-start.2
  4.0 0.0 copy-start.3
  4.0 0.5 fusion.6
  4.5 0.1 reshape.24
  4.6 0.1 copy-done.1
  4.8 0.0 copy-done.2
  4.8 0.0 copy-done.3
  4.8 78.3 %shard_map.91 = bf16[24,96,128]{2,1,0:T(8,128)(2,1)S(1)} custom-call(bf16[24,96,128]{2,1,0:T(8,128)(2,1)S(1)} %fusion.5.own_ref, bf16[25,384]{1,0:T(8,128)(2,1)S(1)} %pad_maximum_fusion.1.pay_ref, bf16[128,256]{1,0:T(8,128)(2,1)S(1)} %pad_maximum_fusion.wqg_ref, bf16[128,256]{1,0:T(8,128)(2,1)S(1)} %slice.11.wkv_ref, f32[1,128]{1,0:T(1,128)S(1)} %bitcast.8, ...), custom_call_target="tpu_custom_call" | custom-call | tf_op jit(solution)/shard_map/pallas_call | solution.py:229
  83.1 0.8 copy.11
  (7 shorter events, 0.0 us)
Async XLA Ops:
  0.0 4.0 %copy-start = (bf16[128,4]{0,1:T(4,128)(2,1)S(1)}, bf16[128,4]{0,1:T(4,128)(2,1)}, u32[]{:S(2)}) copy-start(bf16[128,4]{0,1:T(4,128)(2,1)} %param.15) | copy-start | bytes 3076
  0.0 2.2 %copy-start.4 = (bf16[24,96,128]{2,1,0:T(8,128)(2,1)S(1)}, bf16[24,96,128]{2,1,0:T(8,128)(2,1)}, u32[]{:S(2)}) copy-start(bf16[24,96,128]{2,1,0:T(8,128)(2,1)} %param.9) | copy-start | bytes 1769476
  0.8 2.3 %copy-start.5 = (bf16[128,512]{1,0:T(8,128)(2,1)S(1)}, bf16[128,512]{1,0:T(8,128)(2,1)}, u32[]{:S(2)}) copy-start(bf16[128,512]{1,0:T(8,128)(2,1)} %param.13) | copy-start | bytes 393220
  2.2 0.9 %copy-start.6 = (f32[128]{0:T(128)S(1)}, f32[128]{0:T(128)}, u32[]{:S(2)}) copy-start(f32[128]{0:T(128)} %param.12) | copy-start | bytes 1540
  2.2 0.9 %copy-start.7 = (f32[128]{0:T(128)S(1)}, f32[128]{0:T(128)}, u32[]{:S(2)}) copy-start(f32[128]{0:T(128)} %param.11) | copy-start | bytes 1540
  4.0 0.8 copy-start.1
  4.0 0.8 copy-start.2
  4.0 0.7 copy-start.3

commit v11 on v9

--- a/solution.py
+++ b/solution.py
@@ -6,15 +6,6 @@
 from jax.experimental import pallas as pl
 from jax.experimental.pallas import tpu as pltpu
 from jax.sharding import PartitionSpec as P
-
-
-def layer_norm(pair_block, norm_gain, norm_shift):
-    as_float = pair_block.astype(jnp.float32)
-    center = jnp.mean(as_float, axis=-1, keepdims=True)
-    spread = jnp.mean(jnp.square(as_float - center), axis=-1, keepdims=True)
-    return ((as_float - center) * lax.rsqrt(spread + 1e-05) * norm_gain + norm_shift).astype(
-        jnp.bfloat16
-    )
 
 
 CHUNKS = 8
@@ -52,14 +43,19 @@
 
 def fused_kernel(
     head_count,
-    own_ref,
-    pay_ref,
+    pair_ref,
+    mask_ref,
+    gain_ref,
+    shift_ref,
+    bwt_ref,
     wqg_ref,
     wkv_ref,
     gb_ref,
     ow_ref,
     ob_ref,
     out_ref,
+    own_ref,
+    pay_ref,
     rows_buf,
     pieces,
     bias_buf,
@@ -75,8 +71,8 @@
     group = row_count // col_count
     me_r = lax.axis_index("rows")
     me_c = lax.axis_index("cols")
-    own_rows, width, channels = own_ref.shape
-    depth = pay_ref.shape[0] - 1
+    own_rows, width, channels = pair_ref.shape
+    depth = own_rows
     chunk = own_rows // CHUNKS
     mesh_id = pl.DeviceIdType.MESH
     target_c = me_r // group
@@ -104,6 +100,25 @@
             @pl.when(jnp.logical_not(jnp.logical_and(source == me_r, me_c == c)))
             def _():
                 pl.semaphore_signal(barrier, 1, device_id=(source, c), device_id_type=mesh_id)
+
+    as_float = pair_ref[...].astype(jnp.float32)
+    center = jnp.mean(as_float, axis=-1, keepdims=True)
+    spread = jnp.mean(jnp.square(as_float - center), axis=-1, keepdims=True)
+    normed = (
+        (as_float - center) * lax.rsqrt(spread + 1e-05) * gain_ref[...] + shift_ref[...]
+    ).astype(jnp.bfloat16)
+    own_ref[...] = normed
+    flat = normed.reshape(own_rows * width, channels)
+    bias_t = lax.dot_general(
+        bwt_ref[...], flat, (((1,), (1,)), ((), ())), preferred_element_type=jnp.float32
+    ).astype(jnp.bfloat16)
+    mask_row = mask_ref[...].astype(jnp.float32).astype(jnp.bfloat16)
+    for h in range(head_count):
+        for j in range(own_rows):
+            pay_ref[j : j + 1, h * width : (h + 1) * width] = bias_t[
+                h : h + 1, j * width : (j + 1) * width
+            ]
+        pay_ref[own_rows : own_rows + 1, h * width : (h + 1) * width] = mask_row
 
     pl.semaphore_wait(barrier, col_count + 2 * (half - is_home.astype(jnp.int32)))
 
@@ -217,23 +232,27 @@
             copy.wait_send()
 
 
-def fused(normed, payload, wqg, wkv, gate_bias, out_weight, out_bias, head_count):
-    own_rows, width, channels = normed.shape
+def fused(pair, token_mask, norm_gain, norm_shift, bias_weight, wqg, wkv, gate_bias, out_weight, out_bias):
+    own_rows, width, channels = pair.shape
     cols = lax.axis_size("cols")
     rows = lax.axis_size("rows")
+    head_count = bias_weight.shape[1]
     slots = head_count + 1
-    depth = payload.shape[0] - 1
+    depth = own_rows
     group = rows // cols
     inner = out_weight.shape[0]
     vmem = pl.BlockSpec(memory_space=pltpu.VMEM)
+    payload_shape = (own_rows + 1, head_count * width)
     return pl.pallas_call(
         functools.partial(fused_kernel, head_count),
-        out_shape=jax.ShapeDtypeStruct(normed.shape, jnp.bfloat16),
-        in_specs=[vmem] * 7,
+        out_shape=jax.ShapeDtypeStruct(pair.shape, jnp.bfloat16),
+        in_specs=[vmem] * 10,
         out_specs=vmem,
         scratch_shapes=[
-            pltpu.VMEM((own_rows, cols * width, channels), normed.dtype),
-            pltpu.VMEM((rows,) + payload.shape, payload.dtype),
+            pltpu.VMEM(pair.shape, jnp.bfloat16),
+            pltpu.VMEM(payload_shape, jnp.bfloat16),
+            pltpu.VMEM((own_rows, cols * width, channels), jnp.bfloat16),
+            pltpu.VMEM((rows,) + payload_shape, jnp.bfloat16),
             pltpu.VMEM((slots, group * depth, cols * width), jnp.float32),
             pltpu.SemaphoreType.DMA((CHUNKS, cols)),
             pltpu.SemaphoreType.DMA((CHUNKS,)),
@@ -246,8 +265,11 @@
             has_side_effects=True, collective_id=0, vmem_limit_bytes=48 * 1024 * 1024
         ),
     )(
-        normed,
-        payload,
+        pair,
+        token_mask.reshape(1, width),
+        norm_gain.reshape(1, channels),
+        norm_shift.reshape(1, channels),
+        bias_weight.T,
         wqg,
         wkv,
         gate_bias.reshape(1, inner),
@@ -260,19 +282,11 @@
     pair, token_mask, norm_gain, norm_shift, in_weight, gate_bias, bias_weight, out_weight, out_bias
 ):
     inner = out_weight.shape[0]
-    normed = layer_norm(pair, norm_gain, norm_shift)
-    rows, width, _ = normed.shape
-    head_count = bias_weight.shape[1]
-    bias_tile = jnp.einsum(
-        "jkc,ch->jhk", normed, bias_weight, preferred_element_type=jnp.float32
-    ).astype(jnp.bfloat16)
-    mask_row = jnp.tile(token_mask.astype(jnp.bfloat16), head_count)
-    payload = jnp.concatenate(
-        (bias_tile.reshape(rows, head_count * width), mask_row[None, :]), axis=0
-    )
     wqg = jnp.concatenate((in_weight[:, :inner], in_weight[:, 3 * inner :]), axis=1)
     wkv = in_weight[:, inner : 3 * inner]
-    return fused(normed, payload, wqg, wkv, gate_bias, out_weight, out_bias, head_count)
+    return fused(
+        pair, token_mask, norm_gain, norm_shift, bias_weight, wqg, wkv, gate_bias, out_weight, out_bias
+    )
 
 
 def solution(mesh):

time: 84.9 us -> 82.8 us (0.975)
  other arithmetic: 3.76 us -> 0.01 us
  local copies, waits for them, and re-layouts: 1.21 us -> 3.52 us
    reduce_sum x2 -> x0, other arithmetic: 2.18 us -> none  [the longest x1 1.38 us: layer_norm(): center = jnp.mean(as_float, axis=-1, keepdims=True)]
    unnamed x17 -> x19, local copies, waits for them, and re-layouts: 1 us -> 2.6 us
    convert_element_type x2 -> x0, other arithmetic: 1.55 us -> none  [the longest x1 0.82 us: layer_norm(): ((as_float - center) * lax.rsqrt(spread + 1e-05) * norm_gain + norm_shift...]
    slice x1, local copies, waits for them, and re-layouts: 0.01 us -> 0.92 us  [shards(): wkv = in_weight[:, inner:3 * inner]]
where the time goes in v11:
time: 82.8 us; the launch traced here: 82.6 us
  Pallas kernels  78.9 us (95%)
  local copies, waits for them, and re-layouts  3.52 us (4%)
    pallas_call x1, Pallas kernels, fused(): pl.pallas_call(functools.partial(fused_kernel, head_count), out_shape=jax...  78.9 us
    unnamed x19, local copies, waits for them, and re-layouts  2.6 us

profile of v11, /device:TPU:64, one launch (start us, length us, event | category | flops | bytes accessed | tf_op | source)
XLA Modules:
  0.0 82.6 jit_solution(13073168420874550362)
XLA Ops:
  0.0 0.0 copy-start.8
  0.0 0.9 %slice.11.wkv_ref = bf16[128,256]{1,0:T(8,128)(2,1)S(1)} slice(bf16[128,512]{1,0:T(8,128)(2,1)} %param.13), slice={[0:128], [128:384]} | slice | bytes 131072 | tf_op jit(solution)/shard_map/slice | solution.py:286
  0.9 0.0 copy-done.8
  0.9 0.0 copy-start.1
  0.9 0.0 copy-start.2
  1.0 0.0 copy-start.3
  1.0 0.0 copy-start.4
  1.0 0.0 copy-start.5
  1.0 0.0 copy-start.6
  1.0 0.0 copy-start.7
  1.0 0.7 copy-done.1
  1.7 0.0 copy-done.2
  1.7 0.0 copy-done.3
  1.7 0.0 copy-done.4
  1.7 0.0 copy-done.5
  1.7 0.0 copy-done.6
  1.7 0.0 copy-done.7
  1.7 0.0 copy-start
  1.7 1.1 %copy-done = bf16[24,96,128]{2,1,0:T(8,128)(2,1)S(1)} copy-done((bf16[24,96,128]{2,1,0:T(8,128)(2,1)S(1)}, bf16[24,96,128]{2,1,0:T(8,128)(2,1)}, u32[]{:S(2)}) %copy-start) | copy-done | bytes 589848
  2.8 78.9 %shard_map.91 = bf16[24,96,128]{2,1,0:T(8,128)(2,1)S(1)} custom-call(bf16[24,96,128]{2,1,0:T(8,128)(2,1)S(1)} %copy-done, s32[1,96]{1,0:T(1,128)S(1)} %bitcast.7, f32[1,128]{1,0:T(1,128)S(1)} %bitcast.8, f32[1,128]{1,0:T(1,128)S(1)} %bitcast.9, bf16[4,128]{1,0:T(4,128)(2,1)S(1)} %bitcast.6, bf16[128,256]{1,0:T(8,128)(2,1)S(1)} %pad_maximum_fusion.wqg_ref, ...), custom_call_target="tpu_custom_call" | custom-call | tf_op jit(solution)/shard_map/pallas_call | solution.py:246
  81.8 0.8 copy.11
  (2 shorter events, 0.0 us)
Async XLA Ops:
  0.0 0.9 %copy-start.8 = (bf16[128,512]{1,0:T(8,128)(2,1)S(1)}, bf16[128,512]{1,0:T(8,128)(2,1)}, u32[]{:S(2)}) copy-start(bf16[128,512]{1,0:T(8,128)(2,1)} %param.13) | copy-start | bytes 393220
  0.9 0.8 copy-start.1
  0.9 0.8 copy-start.2
  1.0 0.7 copy-start.3
  1.0 0.7 copy-start.4
  1.0 0.7 copy-start.5
  1.0 0.7 copy-start.6
  1.0 0.7 copy-start.7
  1.7 1.1 %copy-start = (bf16[24,96,128]{2,1,0:T(8,128)(2,1)S(1)}, bf16[24,96,128]{2,1,0:T(8,128)(2,1)}, u32[]{:S(2)}) copy-start(bf16[24,96,128]{2,1,0:T(8,128)(2,1)} %pair_ref.1) | copy-start | bytes 1769476

commit v12 on v11

--- a/solution.py
+++ b/solution.py
@@ -8,7 +8,7 @@
 from jax.sharding import PartitionSpec as P
 
 
-CHUNKS = 8
+CHUNKS = 12
 
 
 def row_update(own, row, bias_ref, masking, wqg, wkv, gb, ow, ob, head_count, head_size):

time: 82.8 us -> 82.1 us (level)
  no operation moved by 1% of the time
where the time goes in v12:
time: 82.1 us; the launch traced here: 81.9 us
  Pallas kernels  78.3 us (95%)
  local copies, waits for them, and re-layouts  3.52 us (4%)
    pallas_call x1, Pallas kernels, fused(): pl.pallas_call(functools.partial(fused_kernel, head_count), out_shape=jax...  78.3 us
    unnamed x19, local copies, waits for them, and re-layouts  2.6 us

profile of v12, /device:TPU:64, one launch (start us, length us, event | category | flops | bytes accessed | tf_op | source)
XLA Modules:
  0.0 81.9 jit_solution(13588196288299395380)
XLA Ops:
  0.0 0.0 copy-start.8
  0.0 0.9 %slice.11.wkv_ref = bf16[128,256]{1,0:T(8,128)(2,1)S(1)} slice(bf16[128,512]{1,0:T(8,128)(2,1)} %param.13), slice={[0:128], [128:384]} | slice | bytes 131072 | tf_op jit(solution)/shard_map/slice | solution.py:286
  0.9 0.0 copy-done.8
  0.9 0.0 copy-start.1
  0.9 0.0 copy-start.2
  1.0 0.0 copy-start.3
  1.0 0.0 copy-start.4
  1.0 0.0 copy-start.5
  1.0 0.0 copy-start.6
  1.0 0.0 copy-start.7
  1.0 0.7 copy-done.1
  1.7 0.0 copy-done.2
  1.7 0.0 copy-done.3
  1.7 0.0 copy-done.4
  1.7 0.0 copy-done.5
  1.7 0.0 copy-done.6
  1.7 0.0 copy-done.7
  1.7 0.0 copy-start
  1.7 1.1 %copy-done = bf16[24,96,128]{2,1,0:T(8,128)(2,1)S(1)} copy-done((bf16[24,96,128]{2,1,0:T(8,128)(2,1)S(1)}, bf16[24,96,128]{2,1,0:T(8,128)(2,1)}, u32[]{:S(2)}) %copy-start) | copy-done | bytes 589848
  2.8 78.3 %shard_map.91 = bf16[24,96,128]{2,1,0:T(8,128)(2,1)S(1)} custom-call(bf16[24,96,128]{2,1,0:T(8,128)(2,1)S(1)} %copy-done, s32[1,96]{1,0:T(1,128)S(1)} %bitcast.7, f32[1,128]{1,0:T(1,128)S(1)} %bitcast.8, f32[1,128]{1,0:T(1,128)S(1)} %bitcast.9, bf16[4,128]{1,0:T(4,128)(2,1)S(1)} %bitcast.6, bf16[128,256]{1,0:T(8,128)(2,1)S(1)} %pad_maximum_fusion.wqg_ref, ...), custom_call_target="tpu_custom_call" | custom-call | tf_op jit(solution)/shard_map/pallas_call | solution.py:246
  81.1 0.8 copy.11
  (2 shorter events, 0.0 us)
Async XLA Ops:
  0.0 0.9 %copy-start.8 = (bf16[128,512]{1,0:T(8,128)(2,1)S(1)}, bf16[128,512]{1,0:T(8,128)(2,1)}, u32[]{:S(2)}) copy-start(bf16[128,512]{1,0:T(8,128)(2,1)} %param.13) | copy-start | bytes 393220
  0.9 0.8 copy-start.1
  0.9 0.8 copy-start.2
  1.0 0.7 copy-start.3
  1.0 0.7 copy-start.4
  1.0 0.7 copy-start.5
  1.0 0.7 copy-start.6
  1.0 0.7 copy-start.7
  1.7 1.1 %copy-start = (bf16[24,96,128]{2,1,0:T(8,128)(2,1)S(1)}, bf16[24,96,128]{2,1,0:T(8,128)(2,1)}, u32[]{:S(2)}) copy-start(bf16[24,96,128]{2,1,0:T(8,128)(2,1)} %pair_ref.1) | copy-start | bytes 1769476

commit v13 on v12

--- a/solution.py
+++ b/solution.py
@@ -54,6 +54,7 @@
     ow_ref,
     ob_ref,
     out_ref,
+    pair_buf,
     own_ref,
     pay_ref,
     rows_buf,
@@ -65,6 +66,7 @@
     bias_send,
     bias_recv,
     fwd_sem,
+    pair_sem,
 ):
     col_count = lax.axis_size("cols")
     row_count = lax.axis_size("rows")
@@ -80,6 +82,8 @@
     parity = lax.rem(me_r, 2)
     half = row_count // 2
     sibling = me_r + 1 - 2 * parity
+    pair_in = pltpu.make_async_copy(pair_ref, pair_buf, pair_sem.at[0])
+    pair_in.start()
     barrier = pltpu.get_barrier_semaphore()
     for p in range(1, col_count):
         pl.semaphore_signal(
@@ -101,7 +105,8 @@
             def _():
                 pl.semaphore_signal(barrier, 1, device_id=(source, c), device_id_type=mesh_id)
 
-    as_float = pair_ref[...].astype(jnp.float32)
+    pair_in.wait()
+    as_float = pair_buf[...].astype(jnp.float32)
     center = jnp.mean(as_float, axis=-1, keepdims=True)
     spread = jnp.mean(jnp.square(as_float - center), axis=-1, keepdims=True)
     normed = (
@@ -246,9 +251,10 @@
     return pl.pallas_call(
         functools.partial(fused_kernel, head_count),
         out_shape=jax.ShapeDtypeStruct(pair.shape, jnp.bfloat16),
-        in_specs=[vmem] * 10,
+        in_specs=[pl.BlockSpec(memory_space=pl.ANY)] + [vmem] * 9,
         out_specs=vmem,
         scratch_shapes=[
+            pltpu.VMEM(pair.shape, pair.dtype),
             pltpu.VMEM(pair.shape, jnp.bfloat16),
             pltpu.VMEM(payload_shape, jnp.bfloat16),
             pltpu.VMEM((own_rows, cols * width, channels), jnp.bfloat16),
@@ -260,6 +266,7 @@
             pltpu.SemaphoreType.DMA((rows // 2,)),
             pltpu.SemaphoreType.DMA(()),
             pltpu.SemaphoreType.DMA((2,)),
+            pltpu.SemaphoreType.DMA((1,)),
         ],
         compiler_params=pltpu.CompilerParams(
             has_side_effects=True, collective_id=0, vmem_limit_bytes=48 * 1024 * 1024

time: 82.1 us -> 82.4 us (level)
  no operation moved by 1% of the time
where the time goes in v13:
time: 82.4 us; the launch traced here: 82.2 us
  Pallas kernels  78.6 us (95%)
  local copies, waits for them, and re-layouts  3.52 us (4%)
    pallas_call x1, Pallas kernels, fused(): pl.pallas_call(functools.partial(fused_kernel, head_count), out_shape=jax...  78.6 us
    unnamed x19, local copies, waits for them, and re-layouts  2.6 us

profile of v13, /device:TPU:64, one launch (start us, length us, event | category | flops | bytes accessed | tf_op | source)
XLA Modules:
  0.0 82.2 jit_solution(1473649665631904162)
XLA Ops:
  0.0 0.0 copy-start.8
  0.0 0.9 %slice.11.wkv_ref = bf16[128,256]{1,0:T(8,128)(2,1)S(1)} slice(bf16[128,512]{1,0:T(8,128)(2,1)} %param.13), slice={[0:128], [128:384]} | slice | bytes 131072 | tf_op jit(solution)/shard_map/slice | solution.py:293
  0.9 0.0 copy-done.8
  0.9 0.0 copy-start.1
  0.9 0.0 copy-start.2
  1.0 0.0 copy-start.3
  1.0 0.0 copy-start.4
  1.0 0.0 copy-start.5
  1.0 0.0 copy-start.6
  1.0 0.0 copy-start.7
  1.0 0.7 copy-done.1
  1.7 0.0 copy-done.2
  1.7 0.0 copy-done.3
  1.7 0.0 copy-done.4
  1.7 0.0 copy-done.5
  1.7 0.0 copy-done.6
  1.7 0.0 copy-done.7
  1.7 0.0 copy-start
  1.7 1.1 %copy-done = bf16[24,96,128]{2,1,0:T(8,128)(2,1)S(1)} copy-done((bf16[24,96,128]{2,1,0:T(8,128)(2,1)S(1)}, bf16[24,96,128]{2,1,0:T(8,128)(2,1)}, u32[]{:S(2)}) %copy-start) | copy-done | bytes 589848
  2.8 78.6 %shard_map.91 = bf16[24,96,128]{2,1,0:T(8,128)(2,1)S(1)} custom-call(bf16[24,96,128]{2,1,0:T(8,128)(2,1)S(1)} %copy-done, s32[1,96]{1,0:T(1,128)S(1)} %bitcast.7, f32[1,128]{1,0:T(1,128)S(1)} %bitcast.8, f32[1,128]{1,0:T(1,128)S(1)} %bitcast.9, bf16[4,128]{1,0:T(4,128)(2,1)S(1)} %bitcast.6, bf16[128,256]{1,0:T(8,128)(2,1)S(1)} %pad_maximum_fusion.wqg_ref, ...), custom_call_target="tpu_custom_call" | custom-call | tf_op jit(solution)/shard_map/pallas_call | solution.py:251
  81.4 0.8 copy.11
  (2 shorter events, 0.0 us)
Async XLA Ops:
  0.0 0.9 %copy-start.8 = (bf16[128,512]{1,0:T(8,128)(2,1)S(1)}, bf16[128,512]{1,0:T(8,128)(2,1)}, u32[]{:S(2)}) copy-start(bf16[128,512]{1,0:T(8,128)(2,1)} %param.13) | copy-start | bytes 393220
  0.9 0.8 copy-start.1
  0.9 0.8 copy-start.2
  1.0 0.7 copy-start.3
  1.0 0.7 copy-start.4
  1.0 0.7 copy-start.5
  1.0 0.7 copy-start.6
  1.0 0.7 copy-start.7
  1.7 1.1 %copy-start = (bf16[24,96,128]{2,1,0:T(8,128)(2,1)S(1)}, bf16[24,96,128]{2,1,0:T(8,128)(2,1)}, u32[]{:S(2)}) copy-start(bf16[24,96,128]{2,1,0:T(8,128)(2,1)} %pair_ref.1) | copy-start | bytes 1769476

commit v14 on v13

--- a/solution.py
+++ b/solution.py
@@ -11,15 +11,18 @@
 CHUNKS = 12
 
 
-def row_update(own, row, bias_ref, masking, wqg, wkv, gb, ow, ob, head_count, head_size):
+def row_update(own, row, bias_ref, masking, w_ref, gb, ow, ob, head_count, head_size):
     inner = head_count * head_size
-    qg = jnp.dot(own, wqg, preferred_element_type=jnp.float32)
-    queries = (qg[:, :inner] * head_size ** (-0.5)).astype(jnp.bfloat16)
-    gates = jax.nn.sigmoid(qg[:, inner:] + gb)
+    qp = jnp.dot(own, w_ref[:, :inner], preferred_element_type=jnp.float32)
+    queries = (qp * head_size ** (-0.5)).astype(jnp.bfloat16)
+    gp = jnp.dot(own, w_ref[:, 3 * inner :], preferred_element_type=jnp.float32)
+    gates = jax.nn.sigmoid(gp + gb)
     keys_t = lax.dot_general(
-        wkv[:, :inner], row, (((0,), (1,)), ((), ())), preferred_element_type=jnp.float32
+        w_ref[:, inner : 2 * inner], row, (((0,), (1,)), ((), ())), preferred_element_type=jnp.float32
     ).astype(jnp.bfloat16)
-    values = jnp.dot(row, wkv[:, inner:], preferred_element_type=jnp.float32).astype(jnp.bfloat16)
+    values = jnp.dot(
+        row, w_ref[:, 2 * inner : 3 * inner], preferred_element_type=jnp.float32
+    ).astype(jnp.bfloat16)
     lane_head = lax.broadcasted_iota(jnp.int32, (1, inner), 1) // head_size
     queries_rows = own.shape[0]
     stacked = jnp.concatenate(
@@ -48,12 +51,13 @@
     gain_ref,
     shift_ref,
     bwt_ref,
-    wqg_ref,
-    wkv_ref,
+    w_hbm,
     gb_ref,
-    ow_ref,
+    ow_hbm,
     ob_ref,
     out_ref,
+    w_ref,
+    ow_ref,
     pair_buf,
     own_ref,
     pay_ref,
@@ -84,6 +88,10 @@
     sibling = me_r + 1 - 2 * parity
     pair_in = pltpu.make_async_copy(pair_ref, pair_buf, pair_sem.at[0])
     pair_in.start()
+    w_in = pltpu.make_async_copy(w_hbm, w_ref, pair_sem.at[1])
+    w_in.start()
+    ow_in = pltpu.make_async_copy(ow_hbm, ow_ref, pair_sem.at[2])
+    ow_in.start()
     barrier = pltpu.get_barrier_semaphore()
     for p in range(1, col_count):
         pl.semaphore_signal(
@@ -197,6 +205,8 @@
                     depth : depth + 1, 0:width
                 ]
     masking = 1000000000.0 * (bias_buf[head_count, 0:1, :] - 1.0)
+    w_in.wait()
+    ow_in.wait()
     inner = ow_ref.shape[0]
     head_size = inner // head_count
 
@@ -215,8 +225,7 @@
                 rows_buf[i],
                 bias_buf,
                 masking,
-                wqg_ref[...],
-                wkv_ref[...],
+                w_ref,
                 gb_ref[...],
                 ow_ref[...],
                 ob_ref[...],
@@ -237,7 +246,7 @@
             copy.wait_send()
 
 
-def fused(pair, token_mask, norm_gain, norm_shift, bias_weight, wqg, wkv, gate_bias, out_weight, out_bias):
+def fused(pair, token_mask, norm_gain, norm_shift, bias_weight, in_weight, gate_bias, out_weight, out_bias):
     own_rows, width, channels = pair.shape
     cols = lax.axis_size("cols")
     rows = lax.axis_size("rows")
@@ -247,13 +256,16 @@
     group = rows // cols
     inner = out_weight.shape[0]
     vmem = pl.BlockSpec(memory_space=pltpu.VMEM)
+    any_spec = pl.BlockSpec(memory_space=pl.ANY)
     payload_shape = (own_rows + 1, head_count * width)
     return pl.pallas_call(
         functools.partial(fused_kernel, head_count),
         out_shape=jax.ShapeDtypeStruct(pair.shape, jnp.bfloat16),
-        in_specs=[pl.BlockSpec(memory_space=pl.ANY)] + [vmem] * 9,
+        in_specs=[any_spec] + [vmem] * 4 + [any_spec, vmem, any_spec, vmem],
         out_specs=vmem,
         scratch_shapes=[
+            pltpu.VMEM(in_weight.shape, in_weight.dtype),
+            pltpu.VMEM(out_weight.shape, out_weight.dtype),
             pltpu.VMEM(pair.shape, pair.dtype),
             pltpu.VMEM(pair.shape, jnp.bfloat16),
             pltpu.VMEM(payload_shape, jnp.bfloat16),
@@ -266,7 +278,7 @@
             pltpu.SemaphoreType.DMA((rows // 2,)),
             pltpu.SemaphoreType.DMA(()),
             pltpu.SemaphoreType.DMA((2,)),
-            pltpu.SemaphoreType.DMA((1,)),
+            pltpu.SemaphoreType.DMA((3,)),
         ],
         compiler_params=pltpu.CompilerParams(
             has_side_effects=True, collective_id=0, vmem_limit_bytes=48 * 1024 * 1024
@@ -277,8 +289,7 @@
         norm_gain.reshape(1, channels),
         norm_shift.reshape(1, channels),
         bias_weight.T,
-        wqg,
-        wkv,
+        in_weight,
         gate_bias.reshape(1, inner),
         out_weight,
         out_bias.reshape(1, channels),
@@ -288,11 +299,8 @@
 def shards(
     pair, token_mask, norm_gain, norm_shift, in_weight, gate_bias, bias_weight, out_weight, out_bias
 ):
-    inner = out_weight.shape[0]
-    wqg = jnp.concatenate((in_weight[:, :inner], in_weight[:, 3 * inner :]), axis=1)
-    wkv = in_weight[:, inner : 3 * inner]
     return fused(
-        pair, token_mask, norm_gain, norm_shift, bias_weight, wqg, wkv, gate_bias, out_weight, out_bias
+        pair, token_mask, norm_gain, norm_shift, bias_weight, in_weight, gate_bias, out_weight, out_bias
     )
 
 

time: 82.4 us -> 83.4 us (1.012)
    unnamed x19, local copies, waits for them, and re-layouts: 2.6 us -> 4.26 us
    slice x2 -> x0, local copies, waits for them, and re-layouts: 0.92 us -> none  [the longest x1 0.92 us: shards(): wkv = in_weight[:, inner:3 * inner]]
where the time goes in v14:
time: 83.4 us; the launch traced here: 83.2 us
  Pallas kernels  78.9 us (95%)
  local copies, waits for them, and re-layouts  4.26 us (5%)
    pallas_call x1, Pallas kernels, fused(): pl.pallas_call(functools.partial(fused_kernel, head_count), out_shape=jax...  78.9 us
    unnamed x19, local copies, waits for them, and re-layouts  4.26 us

profile of v14, /device:TPU:64, one launch (start us, length us, event | category | flops | bytes accessed | tf_op | source)
XLA Modules:
  0.0 83.2 jit_solution(12873767520573141977)
XLA Ops:
  0.0 0.0 copy-start.5
  0.0 0.0 copy-start.6
  0.0 0.0 copy-start.7
  0.0 0.0 copy-start.8
  0.0 0.0 copy-start.3
  0.0 0.0 copy-start.4
  0.0 0.6 copy-done.5
  0.7 0.0 copy-done.6
  0.7 0.0 copy-done.7
  0.7 0.0 copy-done.8
  0.7 0.0 copy-done.3
  0.7 0.0 copy-done.4
  0.7 0.0 copy-start
  0.7 1.1 %copy-done = bf16[24,96,128]{2,1,0:T(8,128)(2,1)S(1)} copy-done((bf16[24,96,128]{2,1,0:T(8,128)(2,1)S(1)}, bf16[24,96,128]{2,1,0:T(8,128)(2,1)}, u32[]{:S(2)}) %copy-start) | copy-done | bytes 589848
  1.8 0.0 copy-start.1
  1.8 0.9 %copy-done.1 = bf16[128,512]{1,0:T(8,128)(2,1)S(1)} copy-done((bf16[128,512]{1,0:T(8,128)(2,1)S(1)}, bf16[128,512]{1,0:T(8,128)(2,1)}, u32[]{:S(2)}) %copy-start.1) | copy-done | bytes 131096
  2.7 0.0 copy-start.2
  2.7 0.8 copy-done.2
  3.5 78.9 %shard_map.91 = bf16[24,96,128]{2,1,0:T(8,128)(2,1)S(1)} custom-call(bf16[24,96,128]{2,1,0:T(8,128)(2,1)S(1)} %copy-done, s32[1,96]{1,0:T(1,128)S(1)} %bitcast.7, f32[1,128]{1,0:T(1,128)S(1)} %bitcast.8, f32[1,128]{1,0:T(1,128)S(1)} %bitcast.9, bf16[4,128]{1,0:T(4,128)(2,1)S(1)} %bitcast.6, bf16[128,512]{1,0:T(8,128)(2,1)S(1)} %copy-done.1, ...), custom_call_target="tpu_custom_call" | custom-call | tf_op jit(solution)/shard_map/pallas_call | solution.py:261
  82.3 0.8 copy.11
Async XLA Ops:
  0.0 0.7 copy-start.5
  0.0 0.7 copy-start.6
  0.0 0.7 copy-start.7
  0.0 0.7 copy-start.8
  0.0 0.7 copy-start.3
  0.0 0.7 copy-start.4
  0.7 1.1 %copy-start = (bf16[24,96,128]{2,1,0:T(8,128)(2,1)S(1)}, bf16[24,96,128]{2,1,0:T(8,128)(2,1)}, u32[]{:S(2)}) copy-start(bf16[24,96,128]{2,1,0:T(8,128)(2,1)} %pair_ref.1) | copy-start | bytes 1769476
  1.8 0.9 %copy-start.1 = (bf16[128,512]{1,0:T(8,128)(2,1)S(1)}, bf16[128,512]{1,0:T(8,128)(2,1)}, u32[]{:S(2)}) copy-start(bf16[128,512]{1,0:T(8,128)(2,1)} %w_hbm.1) | copy-start | bytes 393220
  2.7 0.8 copy-start.2

commit v15 on v14

--- a/solution.py
+++ b/solution.py
@@ -47,15 +47,22 @@
 def fused_kernel(
     head_count,
     pair_ref,
+    mask_hbm,
+    gain_hbm,
+    shift_hbm,
+    bwt_hbm,
+    w_hbm,
+    gb_hbm,
+    ow_hbm,
+    ob_hbm,
+    out_ref,
     mask_ref,
     gain_ref,
     shift_ref,
     bwt_ref,
-    w_hbm,
     gb_ref,
-    ow_hbm,
     ob_ref,
-    out_ref,
+    small_sem,
     w_ref,
     ow_ref,
     pair_buf,
@@ -92,6 +99,20 @@
     w_in.start()
     ow_in = pltpu.make_async_copy(ow_hbm, ow_ref, pair_sem.at[2])
     ow_in.start()
+    small_in = []
+    for n, (src, dst) in enumerate(
+        (
+            (mask_hbm, mask_ref),
+            (gain_hbm, gain_ref),
+            (shift_hbm, shift_ref),
+            (bwt_hbm, bwt_ref),
+            (gb_hbm, gb_ref),
+            (ob_hbm, ob_ref),
+        )
+    ):
+        small = pltpu.make_async_copy(src, dst, small_sem.at[n])
+        small.start()
+        small_in.append(small)
     barrier = pltpu.get_barrier_semaphore()
     for p in range(1, col_count):
         pl.semaphore_signal(
@@ -114,6 +135,8 @@
                 pl.semaphore_signal(barrier, 1, device_id=(source, c), device_id_type=mesh_id)
 
     pair_in.wait()
+    for small in small_in:
+        small.wait()
     as_float = pair_buf[...].astype(jnp.float32)
     center = jnp.mean(as_float, axis=-1, keepdims=True)
     spread = jnp.mean(jnp.square(as_float - center), axis=-1, keepdims=True)
@@ -261,9 +284,16 @@
     return pl.pallas_call(
         functools.partial(fused_kernel, head_count),
         out_shape=jax.ShapeDtypeStruct(pair.shape, jnp.bfloat16),
-        in_specs=[any_spec] + [vmem] * 4 + [any_spec, vmem, any_spec, vmem],
+        in_specs=[any_spec] * 9,
         out_specs=vmem,
         scratch_shapes=[
+            pltpu.VMEM((1, width), token_mask.dtype),
+            pltpu.VMEM((1, channels), norm_gain.dtype),
+            pltpu.VMEM((1, channels), norm_shift.dtype),
+            pltpu.VMEM((head_count, channels), bias_weight.dtype),
+            pltpu.VMEM((1, inner), gate_bias.dtype),
+            pltpu.VMEM((1, channels), out_bias.dtype),
+            pltpu.SemaphoreType.DMA((6,)),
             pltpu.VMEM(in_weight.shape, in_weight.dtype),
             pltpu.VMEM(out_weight.shape, out_weight.dtype),
             pltpu.VMEM(pair.shape, pair.dtype),

time: 83.4 us -> 83.4 us (level)
  no operation moved by 1% of the time
where the time goes in v15:
time: 83.4 us; the launch traced here: 83.2 us
  Pallas kernels  78.9 us (95%)
  local copies, waits for them, and re-layouts  4.26 us (5%)
    pallas_call x1, Pallas kernels, fused(): pl.pallas_call(functools.partial(fused_kernel, head_count), out_shape=jax...  78.9 us
    unnamed x19, local copies, waits for them, and re-layouts  4.26 us

profile of v15, /device:TPU:64, one launch (start us, length us, event | category | flops | bytes accessed | tf_op | source)
XLA Modules:
  0.0 83.2 jit_solution(15608861176870676280)
XLA Ops:
  0.0 0.0 copy-start.5
  0.0 0.0 copy-start.6
  0.0 0.0 copy-start.7
  0.0 0.0 copy-start.8
  0.0 0.0 copy-start.3
  0.0 0.0 copy-start.4
  0.0 0.6 copy-done.5
  0.7 0.0 copy-done.6
  0.7 0.0 copy-done.7
  0.7 0.0 copy-done.8
  0.7 0.0 copy-done.3
  0.7 0.0 copy-done.4
  0.7 0.0 copy-start
  0.7 1.1 %copy-done = bf16[24,96,128]{2,1,0:T(8,128)(2,1)S(1)} copy-done((bf16[24,96,128]{2,1,0:T(8,128)(2,1)S(1)}, bf16[24,96,128]{2,1,0:T(8,128)(2,1)}, u32[]{:S(2)}) %copy-start) | copy-done | bytes 589848
  1.8 0.0 copy-start.1
  1.8 0.9 %copy-done.1 = bf16[128,512]{1,0:T(8,128)(2,1)S(1)} copy-done((bf16[128,512]{1,0:T(8,128)(2,1)S(1)}, bf16[128,512]{1,0:T(8,128)(2,1)}, u32[]{:S(2)}) %copy-start.1) | copy-done | bytes 131096
  2.7 0.0 copy-start.2
  2.7 0.8 copy-done.2
  3.5 78.9 %shard_map.91 = bf16[24,96,128]{2,1,0:T(8,128)(2,1)S(1)} custom-call(bf16[24,96,128]{2,1,0:T(8,128)(2,1)S(1)} %copy-done, s32[1,96]{1,0:T(1,128)S(1)} %bitcast.7, f32[1,128]{1,0:T(1,128)S(1)} %bitcast.8, f32[1,128]{1,0:T(1,128)S(1)} %bitcast.9, bf16[4,128]{1,0:T(4,128)(2,1)S(1)} %bitcast.6, bf16[128,512]{1,0:T(8,128)(2,1)S(1)} %copy-done.1, ...), custom_call_target="tpu_custom_call" | custom-call | tf_op jit(solution)/shard_map/pallas_call | solution.py:284
  82.4 0.8 copy.11
Async XLA Ops:
  0.0 0.7 copy-start.5
  0.0 0.7 copy-start.6
  0.0 0.7 copy-start.7
  0.0 0.7 copy-start.8
  0.0 0.7 copy-start.3
  0.0 0.7 copy-start.4
  0.7 1.1 %copy-start = (bf16[24,96,128]{2,1,0:T(8,128)(2,1)S(1)}, bf16[24,96,128]{2,1,0:T(8,128)(2,1)}, u32[]{:S(2)}) copy-start(bf16[24,96,128]{2,1,0:T(8,128)(2,1)} %pair_ref.1) | copy-start | bytes 1769476
  1.8 0.9 %copy-start.1 = (bf16[128,512]{1,0:T(8,128)(2,1)S(1)}, bf16[128,512]{1,0:T(8,128)(2,1)}, u32[]{:S(2)}) copy-start(bf16[128,512]{1,0:T(8,128)(2,1)} %w_hbm.1) | copy-start | bytes 393220
  2.7 0.8 copy-start.2

commit v16 on v12

--- a/solution.py
+++ b/solution.py
@@ -8,7 +8,7 @@
 from jax.sharding import PartitionSpec as P
 
 
-CHUNKS = 12
+CHUNKS = 24
 
 
 def row_update(own, row, bias_ref, masking, wqg, wkv, gb, ow, ob, head_count, head_size):

time: 82.1 us -> 82 us (level)
  no operation moved by 1% of the time
where the time goes in v16:
time: 82 us; the launch traced here: 81.8 us
  Pallas kernels  78.1 us (95%)
  local copies, waits for them, and re-layouts  3.52 us (4%)
    pallas_call x1, Pallas kernels, fused(): pl.pallas_call(functools.partial(fused_kernel, head_count), out_shape=jax...  78.1 us
    unnamed x19, local copies, waits for them, and re-layouts  2.6 us

profile of v16, /device:TPU:64, one launch (start us, length us, event | category | flops | bytes accessed | tf_op | source)
XLA Modules:
  0.0 81.8 jit_solution(14225531086237755594)
XLA Ops:
  0.0 0.0 copy-start.8
  0.0 0.9 %slice.11.wkv_ref = bf16[128,256]{1,0:T(8,128)(2,1)S(1)} slice(bf16[128,512]{1,0:T(8,128)(2,1)} %param.13), slice={[0:128], [128:384]} | slice | bytes 131072 | tf_op jit(solution)/shard_map/slice | solution.py:286
  0.9 0.0 copy-done.8
  0.9 0.0 copy-start.1
  0.9 0.0 copy-start.2
  1.0 0.0 copy-start.3
  1.0 0.0 copy-start.4
  1.0 0.0 copy-start.5
  1.0 0.0 copy-start.6
  1.0 0.0 copy-start.7
  1.0 0.7 copy-done.1
  1.7 0.0 copy-done.2
  1.7 0.0 copy-done.3
  1.7 0.0 copy-done.4
  1.7 0.0 copy-done.5
  1.7 0.0 copy-done.6
  1.7 0.0 copy-done.7
  1.7 0.0 copy-start
  1.7 1.1 %copy-done = bf16[24,96,128]{2,1,0:T(8,128)(2,1)S(1)} copy-done((bf16[24,96,128]{2,1,0:T(8,128)(2,1)S(1)}, bf16[24,96,128]{2,1,0:T(8,128)(2,1)}, u32[]{:S(2)}) %copy-start) | copy-done | bytes 589848
  2.8 78.1 %shard_map.91 = bf16[24,96,128]{2,1,0:T(8,128)(2,1)S(1)} custom-call(bf16[24,96,128]{2,1,0:T(8,128)(2,1)S(1)} %copy-done, s32[1,96]{1,0:T(1,128)S(1)} %bitcast.7, f32[1,128]{1,0:T(1,128)S(1)} %bitcast.8, f32[1,128]{1,0:T(1,128)S(1)} %bitcast.9, bf16[4,128]{1,0:T(4,128)(2,1)S(1)} %bitcast.6, bf16[128,256]{1,0:T(8,128)(2,1)S(1)} %pad_maximum_fusion.wqg_ref, ...), custom_call_target="tpu_custom_call" | custom-call | tf_op jit(solution)/shard_map/pallas_call | solution.py:246
  80.9 0.8 copy.11
  (2 shorter events, 0.0 us)
Async XLA Ops:
  0.0 0.9 %copy-start.8 = (bf16[128,512]{1,0:T(8,128)(2,1)S(1)}, bf16[128,512]{1,0:T(8,128)(2,1)}, u32[]{:S(2)}) copy-start(bf16[128,512]{1,0:T(8,128)(2,1)} %param.13) | copy-start | bytes 393220
  0.9 0.8 copy-start.1
  0.9 0.8 copy-start.2
  1.0 0.7 copy-start.3
  1.0 0.7 copy-start.4
  1.0 0.7 copy-start.5
  1.0 0.7 copy-start.6
  1.0 0.7 copy-start.7
  1.7 1.1 %copy-start = (bf16[24,96,128]{2,1,0:T(8,128)(2,1)S(1)}, bf16[24,96,128]{2,1,0:T(8,128)(2,1)}, u32[]{:S(2)}) copy-start(bf16[24,96,128]{2,1,0:T(8,128)(2,1)} %pair_ref.1) | copy-start | bytes 1769476

commit v17 on v12

--- a/solution.py
+++ b/solution.py
@@ -179,18 +179,41 @@
         device_id_type=mesh_id,
     )
     forward.start()
+
+    def assemble(blocks):
+        for c in range(col_count):
+            for m in blocks:
+                piece = pieces[(m % 2) * half + (m // 2) * col_count + c].astype(jnp.float32)
+                for h in range(head_count):
+                    bias_buf[h, m * depth : (m + 1) * depth, c * width : (c + 1) * width] = piece[
+                        :depth, h * width : (h + 1) * width
+                    ]
+                if m == 0:
+                    bias_buf[head_count, 0:1, c * width : (c + 1) * width] = piece[
+                        depth : depth + 1, 0:width
+                    ]
+
+    even = [m for m in range(group) if m % 2 == 0]
+    odd = [m for m in range(group) if m % 2 == 1]
+
+    @pl.when(parity == 0)
+    def _():
+        assemble(even)
+
+    @pl.when(parity == 1)
+    def _():
+        assemble(odd)
+
     forward.wait()
-    for c in range(col_count):
-        for m in range(group):
-            piece = pieces[(m % 2) * half + (m // 2) * col_count + c].astype(jnp.float32)
-            for h in range(head_count):
-                bias_buf[h, m * depth : (m + 1) * depth, c * width : (c + 1) * width] = piece[
-                    :depth, h * width : (h + 1) * width
-                ]
-            if m == 0:
-                bias_buf[head_count, 0:1, c * width : (c + 1) * width] = piece[
-                    depth : depth + 1, 0:width
-                ]
+
+    @pl.when(parity == 0)
+    def _():
+        assemble(odd)
+
+    @pl.when(parity == 1)
+    def _():
+        assemble(even)
+
     masking = 1000000000.0 * (bias_buf[head_count, 0:1, :] - 1.0)
     inner = ow_ref.shape[0]
     head_size = inner // head_count

time: 82.1 us -> 82.1 us (level)
  no operation moved by 1% of the time
where the time goes in v17:
time: 82.1 us; the launch traced here: 81.9 us
  Pallas kernels  78.3 us (95%)
  local copies, waits for them, and re-layouts  3.52 us (4%)
    pallas_call x1, Pallas kernels, fused(): pl.pallas_call(functools.partial(fused_kernel, head_count), out_shape=jax...  78.3 us
    unnamed x19, local copies, waits for them, and re-layouts  2.6 us

profile of v17, /device:TPU:64, one launch (start us, length us, event | category | flops | bytes accessed | tf_op | source)
XLA Modules:
  0.0 81.9 jit_solution(17533595459192367593)
XLA Ops:
  0.0 0.0 copy-start.8
  0.0 0.9 %slice.11.wkv_ref = bf16[128,256]{1,0:T(8,128)(2,1)S(1)} slice(bf16[128,512]{1,0:T(8,128)(2,1)} %param.13), slice={[0:128], [128:384]} | slice | bytes 131072 | tf_op jit(solution)/shard_map/slice | solution.py:309
  0.9 0.0 copy-done.8
  0.9 0.0 copy-start.1
  0.9 0.0 copy-start.2
  1.0 0.0 copy-start.3
  1.0 0.0 copy-start.4
  1.0 0.0 copy-start.5
  1.0 0.0 copy-start.6
  1.0 0.0 copy-start.7
  1.0 0.7 copy-done.1
  1.7 0.0 copy-done.2
  1.7 0.0 copy-done.3
  1.7 0.0 copy-done.4
  1.7 0.0 copy-done.5
  1.7 0.0 copy-done.6
  1.7 0.0 copy-done.7
  1.7 0.0 copy-start
  1.7 1.1 %copy-done = bf16[24,96,128]{2,1,0:T(8,128)(2,1)S(1)} copy-done((bf16[24,96,128]{2,1,0:T(8,128)(2,1)S(1)}, bf16[24,96,128]{2,1,0:T(8,128)(2,1)}, u32[]{:S(2)}) %copy-start) | copy-done | bytes 589848
  2.8 78.3 %shard_map.91 = bf16[24,96,128]{2,1,0:T(8,128)(2,1)S(1)} custom-call(bf16[24,96,128]{2,1,0:T(8,128)(2,1)S(1)} %copy-done, s32[1,96]{1,0:T(1,128)S(1)} %bitcast.7, f32[1,128]{1,0:T(1,128)S(1)} %bitcast.8, f32[1,128]{1,0:T(1,128)S(1)} %bitcast.9, bf16[4,128]{1,0:T(4,128)(2,1)S(1)} %bitcast.6, bf16[128,256]{1,0:T(8,128)(2,1)S(1)} %pad_maximum_fusion.wqg_ref, ...), custom_call_target="tpu_custom_call" | custom-call | tf_op jit(solution)/shard_map/pallas_call | solution.py:269
  81.1 0.8 copy.11
  (2 shorter events, 0.0 us)
Async XLA Ops:
  0.0 0.9 %copy-start.8 = (bf16[128,512]{1,0:T(8,128)(2,1)S(1)}, bf16[128,512]{1,0:T(8,128)(2,1)}, u32[]{:S(2)}) copy-start(bf16[128,512]{1,0:T(8,128)(2,1)} %param.13) | copy-start | bytes 393220
  0.9 0.8 copy-start.1
  0.9 0.8 copy-start.2
  1.0 0.7 copy-start.3
  1.0 0.7 copy-start.4
  1.0 0.7 copy-start.5
  1.0 0.7 copy-start.6
  1.0 0.7 copy-start.7
  1.7 1.1 %copy-start = (bf16[24,96,128]{2,1,0:T(8,128)(2,1)S(1)}, bf16[24,96,128]{2,1,0:T(8,128)(2,1)}, u32[]{:S(2)}) copy-start(bf16[24,96,128]{2,1,0:T(8,128)(2,1)} %pair_ref.1) | copy-start | bytes 1769476

commit v18 on v17

--- a/solution.py
+++ b/solution.py
@@ -156,7 +156,7 @@
         local = pltpu.make_async_copy(own_ref.at[part], rows_buf.at[part, home, :], local_sem.at[q])
         local.start()
         locals_.append(local)
-        for p in range(1, col_count):
+        for p in list(range(1, col_count, 2)) + list(range(2, col_count, 2)):
             copy = pltpu.make_async_remote_copy(
                 src_ref=own_ref.at[part],
                 dst_ref=rows_buf.at[part, home, :],

time: 82.1 us -> 82.1 us (level)
  no operation moved by 1% of the time
where the time goes in v18:
time: 82.1 us; the launch traced here: 81.9 us
  Pallas kernels  78.3 us (95%)
  local copies, waits for them, and re-layouts  3.52 us (4%)
    pallas_call x1, Pallas kernels, fused(): pl.pallas_call(functools.partial(fused_kernel, head_count), out_shape=jax...  78.3 us
    unnamed x19, local copies, waits for them, and re-layouts  2.6 us

profile of v18, /device:TPU:64, one launch (start us, length us, event | category | flops | bytes accessed | tf_op | source)
XLA Modules:
  0.0 81.9 jit_solution(14918968223354209501)
XLA Ops:
  0.0 0.0 copy-start.8
  0.0 0.9 %slice.11.wkv_ref = bf16[128,256]{1,0:T(8,128)(2,1)S(1)} slice(bf16[128,512]{1,0:T(8,128)(2,1)} %param.13), slice={[0:128], [128:384]} | slice | bytes 131072 | tf_op jit(solution)/shard_map/slice | solution.py:309
  0.9 0.0 copy-done.8
  0.9 0.0 copy-start.1
  0.9 0.0 copy-start.2
  1.0 0.0 copy-start.3
  1.0 0.0 copy-start.4
  1.0 0.0 copy-start.5
  1.0 0.0 copy-start.6
  1.0 0.0 copy-start.7
  1.0 0.7 copy-done.1
  1.7 0.0 copy-done.2
  1.7 0.0 copy-done.3
  1.7 0.0 copy-done.4
  1.7 0.0 copy-done.5
  1.7 0.0 copy-done.6
  1.7 0.0 copy-done.7
  1.7 0.0 copy-start
  1.7 1.1 %copy-done = bf16[24,96,128]{2,1,0:T(8,128)(2,1)S(1)} copy-done((bf16[24,96,128]{2,1,0:T(8,128)(2,1)S(1)}, bf16[24,96,128]{2,1,0:T(8,128)(2,1)}, u32[]{:S(2)}) %copy-start) | copy-done | bytes 589848
  2.8 78.3 %shard_map.91 = bf16[24,96,128]{2,1,0:T(8,128)(2,1)S(1)} custom-call(bf16[24,96,128]{2,1,0:T(8,128)(2,1)S(1)} %copy-done, s32[1,96]{1,0:T(1,128)S(1)} %bitcast.7, f32[1,128]{1,0:T(1,128)S(1)} %bitcast.8, f32[1,128]{1,0:T(1,128)S(1)} %bitcast.9, bf16[4,128]{1,0:T(4,128)(2,1)S(1)} %bitcast.6, bf16[128,256]{1,0:T(8,128)(2,1)S(1)} %pad_maximum_fusion.wqg_ref, ...), custom_call_target="tpu_custom_call" | custom-call | tf_op jit(solution)/shard_map/pallas_call | solution.py:269
  81.1 0.8 copy.11
  (2 shorter events, 0.0 us)
Async XLA Ops:
  0.0 0.9 %copy-start.8 = (bf16[128,512]{1,0:T(8,128)(2,1)S(1)}, bf16[128,512]{1,0:T(8,128)(2,1)}, u32[]{:S(2)}) copy-start(bf16[128,512]{1,0:T(8,128)(2,1)} %param.13) | copy-start | bytes 393220
  0.9 0.8 copy-start.1
  0.9 0.8 copy-start.2
  1.0 0.7 copy-start.3
  1.0 0.7 copy-start.4
  1.0 0.7 copy-start.5
  1.0 0.7 copy-start.6
  1.0 0.7 copy-start.7
  1.7 1.1 %copy-start = (bf16[24,96,128]{2,1,0:T(8,128)(2,1)S(1)}, bf16[24,96,128]{2,1,0:T(8,128)(2,1)}, u32[]{:S(2)}) copy-start(bf16[24,96,128]{2,1,0:T(8,128)(2,1)} %pair_ref.1) | copy-start | bytes 1769476
